TPU v7x, 32 devices: a whole 2x2x4 slice. The times are simulated.
32 devices in a mesh: lat: 8 (over z, y), lev: 4 (over x, core).
Axes of the slice: x: 2, y: 2, z: 4, core: 2. Of those that a mesh axis runs over, the one named last changes fastest.
Arguments:
- field: float32 [4, 320, 4096], P(None, 'lat', 'lev'), may hold values from -6 to 6
- weights: bfloat16 [4, 320, 4096], P(None, 'lat', 'lev'), may hold values from 0 to 0.5
- depart_row: int32 [320, 4096], P('lat', 'lev'), may hold values from -2 to 1
- depart_col: int32 [320, 4096], P('lat', 'lev'), may hold values from -2 to 1
- legendre: bfloat16 [320, 16, 640], P('lat'), may hold values from -6 to 6
- wave_slot: int32 [16], replicated, may hold values from 0 to 15, each once
Outputs:
- updated: float32 [4, 320, 4096], P(None, 'lat', 'lev')
- spectral: float32 [16, 2, 4, 2, 640], P('lat', None, 'lev')
Inputs may be any that keep to these rules, and one draw needn't show every extreme that they name: `depart_row`: latitude offsets of departure cells, so that rows i - 2 to i + 2 are read. `depart_col`: longitude offsets of departure cells, so that columns j - 2 to j + 2 are read, periodically. `wave_slot`: A permutation of 0 to 15.
All inputs are finite; a program needn't handle non-finite values.
Results may differ from a plain program's by a relative error of at most 0.0033.
Values may be sent and summed in bfloat16 or wider, within the bound.
A program may use at most 128 MiB of HBM per device.

v0:
```python
import functools
import math

import jax
import jax.numpy as jnp
import numpy as np
from jax import lax
from jax.experimental import pallas as pl
from jax.experimental.pallas import tpu as pltpu
from jax.sharding import PartitionSpec as P

NLON = 4096
NT = 1279
DAMPING = 4.0
LANES = 128
HALF = 64
MESH = pl.DeviceIdType.MESH
F32 = jnp.float32
BF16 = jnp.bfloat16


def lon_table(waves):
    m = (np.arange(waves, dtype=np.int64) * (NT + 1)) // waves
    phases = (m[:, None] * np.arange(NLON, dtype=np.int64)[None, :]) % NLON
    angles = phases.astype(np.float64) * (2.0 * math.pi / NLON)
    table = np.concatenate([np.cos(angles), -np.sin(angles)], axis=0) / math.sqrt(NLON)
    table = table.astype(np.float32)
    lead = table.astype(BF16)
    rest = (table - lead.astype(np.float32)).astype(BF16)
    return np.concatenate([lead, rest], axis=0)


def kernel(
    n_lat, n_lev,
    slot_ref, field_hbm, weights_hbm, drow_hbm, dcol_hbm, leg_hbm, table_hbm,
    out_ref, spec_ref,
    ext, shifted, wts, drow, dcol, leg, tab, adv, inv,
    pack_row, pack_col, got_row, got_col, got_corner,
    send_f, got_f, send_x, got_x, sums, send_s, got_s, send_c, got_c,
    chg_slot, chg, send_h, got_h,
    load_sem, halo_send, halo_recv, f_send, f_recv, x_send, x_recv,
    s_send, s_recv, c_send, c_recv, h_send, h_recv,
):
    levels, rows, width = out_ref.shape
    tiles = width // LANES
    waves, steps = leg.shape[1], leg.shape[2]
    l, e = lax.axis_index("lat"), lax.axis_index("lev")
    mirror = n_lat - 1 - l
    has_up, has_down = l > 0, l < n_lat - 1
    east, west = lax.rem(e + 1, n_lev), lax.rem(e + n_lev - 1, n_lev)
    others = lambda start, size: [lax.rem(start + off, size) for off in range(1, size)]

    loads = []

    def load(src, dst):
        copy = pltpu.make_async_copy(src, dst, load_sem.at[len(loads)])
        copy.start()
        loads.append(copy)

    for t in range(tiles):
        load(
            field_hbm.at[:, :, pl.ds(t * LANES, LANES)],
            ext.at[:, t + 1, pl.ds(8, rows), :],
        )
    load(weights_hbm, wts)
    load(drow_hbm, drow)
    load(dcol_hbm, dcol)
    load(table_hbm.at[:, pl.ds(pl.multiple_of(e * width, LANES), width)], tab)
    load(leg_hbm, leg)

    barrier = pltpu.get_barrier_semaphore()

    def greet(lat, lev):
        pl.semaphore_signal(barrier, inc=1, device_id=(lat, lev), device_id_type=MESH)

    for d in others(l, n_lat):
        greet(d, e)
    for d in others(e, n_lev):
        greet(l, d)
        greet(mirror, d)

    @pl.when(has_up)
    def _():
        greet(l - 1, east)
        greet(l - 1, west)

    @pl.when(has_down)
    def _():
        greet(l + 1, east)
        greet(l + 1, west)

    lane = lax.broadcasted_iota(jnp.int32, (rows, LANES), 1)
    for t in range(tiles):
        loads[t].wait()
    for v in range(levels):
        for t in range(tiles):
            cols = slice(t * LANES, (t + 1) * LANES)
            pack_row[0, 2 * v : 2 * v + 2, cols] = ext[v, t + 1, 6 + rows : 8 + rows, :]
            pack_row[1, 2 * v : 2 * v + 2, cols] = ext[v, t + 1, 8:10, :]
    last = jnp.zeros((rows, LANES), F32)
    first = jnp.zeros((rows, LANES), F32)
    for v in range(levels):
        here = (lane == 2 * v) | (lane == 2 * v + 1)
        tail = pltpu.roll(ext[v, tiles, 8 : 8 + rows, :], (2 * v + 2) % LANES, 1)
        last = jnp.where(here, tail, last)
        head = ext[v, 1, 8 : 8 + rows, :]
        if v:
            head = pltpu.roll(head, 2 * v, 1)
        first = jnp.where(here, head, first)
    pack_col[0] = last
    pack_col[1] = first

    def shift_block(v, t, row0, size, moves=(-2, -1, 1, 2)):
        at = pl.ds(row0, size)
        at_lane = lax.broadcasted_iota(jnp.int32, (size, LANES), 1)
        here = ext[v, t + 1, at, :]
        left = ext[v, t, at, :] if min(moves) < 0 else None
        right = ext[v, t + 2, at, :] if max(moves) > 0 else None
        for move in moves:
            n_move = (-2, -1, 1, 2).index(move)
            amount = (-move) % LANES
            mine = pltpu.roll(here, amount, 1)
            if move < 0:
                moved = jnp.where(at_lane < -move, pltpu.roll(left, amount, 1), mine)
            else:
                moved = jnp.where(at_lane >= LANES - move, pltpu.roll(right, amount, 1), mine)
            shifted[n_move, v, t, at, :] = moved

    def shift_inner(chosen):
        def step(t, carry):
            for v in chosen:
                shift_block(v, t, 8, rows)
            return carry

        lax.fori_loop(1, tiles - 1, step, 0)

    groups = rows // 8

    def advect(t, chosen):
        cols = pl.ds(pl.multiple_of(t * LANES, LANES), LANES)
        corner = [wts[ab, :, cols].astype(F32) for ab in range(4)]
        for g in chosen:
            band = slice(8 * g, 8 * g + 8)
            dr, dc = drow[band, cols], dcol[band, cols]
            zero = jnp.zeros((8, LANES), F32)
            in_col = {c: dc == c for c in range(-2, 2)}
            in_row = {r: dr == r for r in range(-2, 2)}

            def pick(masks, at, one, two):
                value = zero
                if at - 1 in masks:
                    value = jnp.where(masks[at - 1], two, value)
                if at in masks:
                    value = jnp.where(masks[at], one, value)
                return value

            part = [
                [pick(in_col, c, corner[2 * a][band], corner[2 * a + 1][band]) for c in range(-2, 3)]
                for a in range(2)
            ]
            coef = [
                [pick(in_row, r, part[0][c], part[1][c]) for c in range(5)] for r in range(-2, 3)
            ]
            for v in range(levels):
                total = None
                for r in range(5):
                    at = pl.ds(8 * g + 6 + r, 8)
                    for c in range(5):
                        if c == 2:
                            value = ext[v, t + 1, at, :]
                        else:
                            value = shifted[c if c < 2 else c - 1, v, t, at, :]
                        term = coef[r][c] * value
                        total = term if total is None else total + term
                adv[v * rows + 8 * g : v * rows + 8 * g + 8, cols] = total

    def advect_inner(t, carry):
        advect(t, range(1, groups - 1))
        return carry

    shift_inner(range(levels // 2))

    n_greet = (n_lat - 1) + 2 * (n_lev - 1)
    n_greet = n_greet + jnp.where(has_up, 2, 0) + jnp.where(has_down, 2, 0)
    pl.semaphore_wait(barrier, n_greet)

    def remote(src, dst, ssem, rsem, lat, lev):
        return pltpu.make_async_remote_copy(
            src_ref=src, dst_ref=dst, send_sem=ssem, recv_sem=rsem,
            device_id=(lat, lev), device_id_type=MESH,
        )

    def halo(n, src, dst, lat, lev):
        return remote(src, dst, halo_send.at[n], halo_recv.at[n], lat, lev)

    bottom, top = pl.ds(rows - 8, 8), pl.ds(0, 8)
    flat = [
        halo(0, pack_col.at[0], got_col.at[0], l, east),
        halo(1, pack_col.at[1], got_col.at[1], l, west),
    ]
    below = [
        halo(2, pack_row.at[0], got_row.at[0], l + 1, e),
        halo(3, pack_col.at[0, bottom], got_corner.at[0], l + 1, east),
        halo(4, pack_col.at[1, bottom], got_corner.at[1], l + 1, west),
    ]
    above = [
        halo(5, pack_row.at[1], got_row.at[1], l - 1, e),
        halo(6, pack_col.at[0, top], got_corner.at[2], l - 1, east),
        halo(7, pack_col.at[1, top], got_corner.at[3], l - 1, west),
    ]

    @pl.when(has_down)
    def _():
        for copy in below:
            copy.start()

    @pl.when(has_up)
    def _():
        for copy in above:
            copy.start()

    for copy in flat:
        copy.start()

    def find(s, carry):
        def step(k, found):
            return jnp.where(slot_ref[k] == s, k, found)

        inv[s] = lax.fori_loop(0, waves, step, jnp.int32(0))
        return carry

    lax.fori_loop(0, waves, find, 0)

    shift_inner(range(levels // 2, levels))
    if tiles > 1:
        for v in range(levels):
            shift_block(v, 0, 8, rows, (1, 2))
            shift_block(v, tiles - 1, 8, rows, (-2, -1))
    for n in range(tiles, tiles + 3):
        loads[n].wait()
    lax.fori_loop(1, tiles - 1, advect_inner, 0)

    def spread(piece, v):
        return pltpu.roll(piece, LANES - 2 - 2 * v, 1)

    def spread_east(piece, v):
        return pltpu.roll(piece, LANES - 2 * v, 1) if v else piece

    def rim(row0, size, from_west, from_east):
        for v in range(levels):
            ext[v, 0, row0 : row0 + size, :] = spread(from_west, v)
            ext[v, tiles + 1, row0 : row0 + size, :] = spread_east(from_east, v)

    def fill_rows(which, row0):
        for v in range(levels):
            for t in range(tiles):
                cols = slice(t * LANES, (t + 1) * LANES)
                ext[v, t + 1, row0 : row0 + 2, :] = got_row[which, 2 * v : 2 * v + 2, cols]

    @pl.when(has_up)
    def _():
        for copy in below:
            copy.wait_recv()
        fill_rows(0, 6)
        rim(0, 8, got_corner[0], got_corner[1])

    @pl.when(jnp.logical_not(has_up))
    def _():
        ext[:, :, 0:8, :] = jnp.zeros((levels, tiles + 2, 8, LANES), F32)

    @pl.when(has_down)
    def _():
        for copy in above:
            copy.wait_recv()
        fill_rows(1, rows + 8)
        rim(rows + 8, 8, got_corner[2], got_corner[3])

    @pl.when(jnp.logical_not(has_down))
    def _():
        ext[:, :, rows + 8 : rows + 16, :] = jnp.zeros((levels, tiles + 2, 8, LANES), F32)

    for copy in flat:
        copy.wait_recv()
    rim(8, rows, got_col[0], got_col[1])

    def shift_rims(t, carry):
        for v in range(levels):
            shift_block(v, t, 0, 8)
            shift_block(v, t, rows + 8, 8)
        return carry

    edges = min(tiles, 2)
    for v in range(levels):
        shift_block(v, 0, 8, rows, (-2, -1))
        shift_block(v, tiles - 1, 8, rows, (1, 2))
    lax.fori_loop(0, tiles, shift_rims, 0)
    outer = sorted({0, groups - 1})

    def advect_rims(t, carry):
        advect(t, outer)
        return carry

    def advect_edge(n, carry):
        advect(n * (tiles - 1), range(groups))
        return carry

    lax.fori_loop(0, edges, advect_edge, 0)
    lax.fori_loop(1, tiles - 1, advect_rims, 0)

    loads[tiles + 3].wait()
    contract_last = (((1,), (1,)), ((), ()))
    send_f[...] = jnp.zeros_like(send_f)
    for v in range(levels):
        value = adv[v * rows : (v + 1) * rows, :]
        lead = value.astype(BF16)
        rest = (value - lead.astype(F32)).astype(BF16)
        both = lax.dot_general(tab[...], lead, contract_last, preferred_element_type=F32)
        more = lax.dot_general(
            tab[0 : 2 * waves, :], rest, contract_last, preferred_element_type=F32
        )
        coeffs = both[0 : 2 * waves] + both[2 * waves :] + more
        send_f[v, :, 0:rows] = coeffs[0:waves]
        send_f[v, :, HALF : HALF + rows] = coeffs[waves:]
    copies_f = []
    for d in others(e, n_lev):
        copy = remote(send_f.at[d], got_f.at[e], f_send.at[d], f_recv.at[e], l, d)
        copy.start()
        copies_f.append(copy)
    got_f[e] = send_f[e]
    for d in others(e, n_lev):
        remote(send_f.at[d], got_f.at[d], f_send.at[d], f_recv.at[d], l, d).wait_recv()
    total = got_f[0]
    for d in range(1, n_lev):
        total = total + got_f[d]
    fourier = total.astype(BF16)
    send_x[...] = fourier
    copy_x = remote(send_x, got_x, x_send, x_recv, mirror, e)
    copy_x.start()

    at_row = lax.broadcasted_iota(jnp.int32, (LANES, LANES), 0)
    at_col = lax.broadcasted_iota(jnp.int32, (LANES, LANES), 1)
    flip = ((at_row + at_col == rows - 1) & (at_row < HALF) & (at_col < HALF)) | (
        (at_row + at_col == 2 * HALF + rows - 1) & (at_row >= HALF) & (at_col >= HALF)
    )
    flip = flip.astype(F32)
    sign = jnp.where(l < n_lat // 2, 1.0, -1.0).astype(F32)
    loads[tiles + 4].wait()
    copy_x.wait_recv()
    partner = jnp.dot(got_x[...], flip.astype(BF16), preferred_element_type=F32)
    combined = partner + sign * fourier.astype(F32)

    forward_scale = 1.0 / math.sqrt(rows * n_lat // 2)
    group = 16
    for k0 in range(0, waves, group):
        ks = slice(k0, k0 + group)
        real = jnp.zeros((group, steps), F32)
        imag = jnp.zeros((group, steps), F32)
        for i in range(rows):
            values = leg[i, ks, :].astype(F32)
            real = real + values * combined[ks, i : i + 1]
            imag = imag + values * combined[ks, HALF + i : HALF + i + 1]
        sums[0, ks, :] = real * forward_scale
        sums[1, ks, :] = imag * forward_scale
    for s in range(waves):
        k = inv[s]
        chg_slot[s, 0:1, :] = sums[0, pl.ds(k, 1), :]
        chg_slot[s, 1:2, :] = sums[1, pl.ds(k, 1), :]
    send_s[...] = chg_slot[...]
    own = waves // n_lat
    copies_s = []
    for d in others(l, n_lat):
        copy = remote(
            send_s.at[pl.ds(d * own, own)], got_s.at[l], s_send.at[d], s_recv.at[l], d, e
        )
        copy.start()
        copies_s.append(copy)
    got_s[l] = send_s[pl.ds(l * own, own)]
    for d in others(l, n_lat):
        remote(
            send_s.at[pl.ds(d * own, own)], got_s.at[d], s_send.at[d], s_recv.at[d], d, e
        ).wait_recv()

    column = lax.broadcasted_iota(jnp.int32, (2, steps), 1)
    for p in range(2):
        start = p * (n_lat // 2)
        raw = got_s[start]
        for d in range(start + 1, start + n_lat // 2):
            raw = raw + got_s[d]
        for so in range(own):
            wave = inv[l * own + so] * (NT + 1) // waves
            degree = wave + 2 * column + p
            factor = 1.0 / (
                1.0 + DAMPING * (degree * (degree + 1)).astype(F32) / float(NT * (NT + 1))
            )
            masked = jnp.where(degree <= NT, raw[so], 0.0)
            damped = masked * factor
            spec_ref[so, p, 0] = damped
            send_c[p, so] = (damped - masked).astype(BF16)
    copies_c = []
    parity_of = lambda d: d // (n_lat // 2)
    for d in others(l, n_lat):
        copy = remote(send_c.at[parity_of(d)], got_c.at[l], c_send.at[d], c_recv.at[l], d, e)
        copy.start()
        copies_c.append(copy)
    got_c[l] = send_c[parity_of(l)]
    for d in others(l, n_lat):
        remote(
            send_c.at[parity_of(d)], got_c.at[d], c_send.at[d], c_recv.at[d], d, e
        ).wait_recv()

    for d in range(n_lat):
        for so in range(own):
            chg_slot[d * own + so] = got_c[d, so].astype(F32)
    for k in range(waves):
        value = chg_slot[slot_ref[k]]
        chg[0, k : k + 1, :] = value[0:1]
        chg[1, k : k + 1, :] = value[1:2]
    inverse_scale = math.sqrt(NLON) / math.sqrt(waves) / math.sqrt(steps)
    lane = lax.broadcasted_iota(jnp.int32, (group, LANES), 1)
    wave_row = lax.broadcasted_iota(jnp.int32, (group, LANES), 0)
    for k0 in range(0, waves, group):
        ks = slice(k0, k0 + group)
        real, imag = chg[0, ks, :], chg[1, ks, :]
        half = jnp.zeros((group, LANES), F32)
        for i in range(rows):
            values = leg[i, ks, :].astype(F32)
            half = jnp.where(lane == i, jnp.sum(values * real, axis=1, keepdims=True), half)
            half = jnp.where(
                lane == HALF + i, jnp.sum(values * imag, axis=1, keepdims=True), half
            )
        half = half * jnp.where(wave_row + k0 == 0, inverse_scale, 2.0 * inverse_scale)
        send_h[0, ks, :] = half
        send_h[1, ks, :] = jnp.dot(
            half, flip, precision=lax.Precision.HIGHEST, preferred_element_type=F32
        )
    copies_h = []
    for off in range(n_lev):
        d = lax.rem(e + off, n_lev)
        copy = remote(send_h.at[1], got_h.at[1, e], h_send.at[1, d], h_recv.at[1, e], mirror, d)
        copy.start()
        copies_h.append(copy)
    for d in others(e, n_lev):
        copy = remote(send_h.at[0], got_h.at[0, e], h_send.at[0, d], h_recv.at[0, e], l, d)
        copy.start()
        copies_h.append(copy)
    got_h[0, e] = send_h[0]
    for d in others(e, n_lev):
        remote(
            send_h.at[0], got_h.at[0, d], h_send.at[0, d], h_recv.at[0, d], l, d
        ).wait_recv()
    for off in range(n_lev):
        d = lax.rem(e + off, n_lev)
        remote(
            send_h.at[1], got_h.at[1, d], h_send.at[1, d], h_recv.at[1, d], mirror, d
        ).wait_recv()

    stack = []
    for v in range(levels):
        synthesis = got_h[1, v] + sign * got_h[0, v]
        both = jnp.concatenate([synthesis, pltpu.roll(synthesis, HALF, 1)], axis=0)
        stack.append(jnp.transpose(both)[0:rows, :])
    synthesis = jnp.concatenate(stack, axis=0)
    lead = synthesis.astype(BF16)
    rest = (synthesis - lead.astype(F32)).astype(BF16)
    chunk = min(width, 256)
    for j in range(0, width, chunk):
        cols = slice(j, j + chunk)
        table, table_rest = tab[0 : 2 * waves, cols], tab[2 * waves :, cols]
        increment = (
            jnp.dot(lead, table, preferred_element_type=F32)
            + jnp.dot(lead, table_rest, preferred_element_type=F32)
            + jnp.dot(rest, table, preferred_element_type=F32)
        )
        updated = adv[:, cols] + increment
        for v in range(levels):
            out_ref[v, :, cols] = updated[v * rows : (v + 1) * rows]

    for copy in flat + copies_f + [copy_x] + copies_s + copies_c + copies_h:
        copy.wait_send()

    @pl.when(has_down)
    def _():
        for copy in below:
            copy.wait_send()

    @pl.when(has_up)
    def _():
        for copy in above:
            copy.wait_send()


def solution(mesh):
    n_lat, n_lev = mesh.shape["lat"], mesh.shape["lev"]

    def on_device(field, weights, depart_row, depart_col, legendre, wave_slot):
        levels, rows, width = field.shape
        _, waves, steps = legendre.shape
        tiles = width // LANES
        own = waves // n_lat
        table = jnp.asarray(lon_table(waves))
        vmem, dma = pltpu.VMEM, pltpu.SemaphoreType.DMA
        anywhere = pl.BlockSpec(memory_space=pltpu.HBM)
        in_vmem = pl.BlockSpec(memory_space=pltpu.VMEM)
        return pl.pallas_call(
            functools.partial(kernel, n_lat, n_lev),
            out_shape=(
                jax.ShapeDtypeStruct((levels, rows, width), F32),
                jax.ShapeDtypeStruct((own, 2, 1, 2, steps), F32),
            ),
            in_specs=[pl.BlockSpec(memory_space=pltpu.SMEM)] + [anywhere] * 6,
            out_specs=(in_vmem, in_vmem),
            scratch_shapes=[
                vmem((levels, tiles + 2, rows + 16, LANES), F32),
                vmem((4, levels, tiles, rows + 16, LANES), F32),
                vmem((4, rows, width), BF16),
                vmem((rows, width), jnp.int32),
                vmem((rows, width), jnp.int32),
                vmem((rows, waves, steps), BF16),
                vmem((4 * waves, width), BF16),
                vmem((levels * rows, width), F32),
                pltpu.SMEM((waves,), jnp.int32),
                vmem((2, 2 * levels, width), F32),
                vmem((2, rows, LANES), F32),
                vmem((2, 2 * levels, width), F32),
                vmem((2, rows, LANES), F32),
                vmem((4, 8, LANES), F32),
                vmem((n_lev, waves, LANES), F32),
                vmem((n_lev, waves, LANES), F32),
                vmem((waves, LANES), BF16),
                vmem((waves, LANES), BF16),
                vmem((2, waves, steps), F32),
                vmem((waves, 2, steps), F32),
                vmem((n_lat, own, 2, steps), F32),
                vmem((2, own, 2, steps), BF16),
                vmem((n_lat, own, 2, steps), BF16),
                vmem((waves, 2, steps), F32),
                vmem((2, waves, steps), F32),
                vmem((2, waves, LANES), F32),
                vmem((2, n_lev, waves, LANES), F32),
                dma((tiles + 5,)),
                dma((8,)), dma((8,)),
                dma((n_lev,)), dma((n_lev,)),
                dma, dma,
                dma((n_lat,)), dma((n_lat,)),
                dma((n_lat,)), dma((n_lat,)),
                dma((2, n_lev)), dma((2, n_lev)),
            ],
            compiler_params=pltpu.CompilerParams(
                collective_id=0, has_side_effects=True, vmem_limit_bytes=63 << 20
            ),
        )(wave_slot, field, weights, depart_row, depart_col, legendre, table)

    placed = (
        P(None, "lat", "lev"),
        P(None, "lat", "lev"),
        P("lat", "lev"),
        P("lat", "lev"),
        P("lat", None, None),
        P(),
    )
    return jax.shard_map(
        on_device,
        mesh=mesh,
        in_specs=placed,
        out_specs=(P(None, "lat", "lev"), P("lat", None, "lev", None, None)),
        check_vma=False,
    )
```

profile of v0, /device:TPU:0, one launch (start us, length us, event | category | flops | bytes accessed | tf_op | source)
XLA Modules:
  0.0 39.6 jit_solution(9359505329240801094)
XLA Ops:
  0.6 36.4 %shard_map.86 = (f32[4,40,1024]{2,1,0:T(8,128)}, f32[2,2,1,2,640]{4,3,2,1,0:T(2,128)}) custom-call(s32[16]{0:T(128)} %slot_ref.1, f32[4,40,1024]{2,1,0:T(8,128)} %field_hbm.1, bf16[4,40,1024]{2,1,0:T(8,128)(2,1)} %weights_hbm.1, s32[40,1024]{1,0:T(8,128)} %drow_hbm.1, s32[40,1024]{1,0:T(8,128)} %dcol_hbm.1, bf16[40,16,640]{2,1,0:T(8,128)(2,1)} %leg_hbm.1, ...), custom_call_target="tpu_custom_call" | custom-call | tf_op jit(solution)/shard_map/pallas_call | solution.py:504
  37.0 0.0 copy-start
  37.0 2.0 %copy.11 = f32[4,40,1024]{2,1,0:T(8,128)} copy(f32[4,40,1024]{2,1,0:T(8,128)} %get-tuple-element.4) | data formatting | bytes 1310720
  39.0 0.0 copy-done
  39.0 0.6 %copy.12 = f32[2,2,1,2,640]{4,3,2,1,0:T(2,128)} copy(f32[2,2,1,2,640]{4,3,2,1,0:T(2,128)S(1)} %copy-done) | data formatting | bytes 40960
Async XLA Ops:
  37.0 2.0 %copy-start = (f32[2,2,1,2,640]{4,3,2,1,0:T(2,128)S(1)}, f32[2,2,1,2,640]{4,3,2,1,0:T(2,128)}, u32[]{:S(2)}) copy-start(f32[2,2,1,2,640]{4,3,2,1,0:T(2,128)} %get-tuple-element.5) | copy-start | bytes 61444
where the time goes:
time: 39.8 us; the launch traced here: 39.6 us
  Pallas kernels  36.4 us (91%)
  local copies, waits for them, and re-layouts  2.6 us (7%)
  between operations  0.65 us (2%)
    pallas_call x1, Pallas kernels, on_device(): pl.pallas_call(functools.partial(kernel, n_lat, n_lev), out_shape=(jax.Sh...  36.4 us
    unnamed x4, local copies, waits for them, and re-layouts  2.6 us

commit v1 on v0

v1 whole, which is shorter than its diff:
```python
import functools
import math

import jax
import jax.numpy as jnp
import numpy as np
from jax import lax
from jax.experimental import pallas as pl
from jax.experimental.pallas import tpu as pltpu
from jax.sharding import PartitionSpec as P

NLON = 4096
NT = 1279
DAMPING = 4.0
LANES = 128
HALF = 64
MESH = pl.DeviceIdType.MESH
F32 = jnp.float32
BF16 = jnp.bfloat16


def lon_table(waves):
    m = (np.arange(waves, dtype=np.int64) * (NT + 1)) // waves
    phases = (m[:, None] * np.arange(NLON, dtype=np.int64)[None, :]) % NLON
    angles = phases.astype(np.float64) * (2.0 * math.pi / NLON)
    table = np.concatenate([np.cos(angles), -np.sin(angles)], axis=0) / math.sqrt(NLON)
    table = table.astype(np.float32)
    lead = table.astype(BF16)
    rest = (table - lead.astype(np.float32)).astype(BF16)
    return np.concatenate([lead, rest], axis=0)


def each(start, stop):
    def run(body):
        if stop - start <= 64:
            for i in range(start, stop):
                body(i)
        else:
            lax.fori_loop(start, stop, lambda i, carry: (body(i), carry)[1], 0)

    return run


def one_hot(mask):
    return jnp.where(mask, 1.0, 0.0).astype(BF16)


def kernel(
    n_lat, n_lev,
    slot_ref, field_hbm, weights_hbm, drow_hbm, dcol_hbm, leg_hbm, table_hbm,
    adv, synth, wide, spec_ref,
    ext, shifted, wts, drow, dcol, leg, tab, tabs,
    pack_row, pack_col, got_row, got_col, got_corner,
    send_leg, basis, stage, send_1, got_1, both_f, both_b, send_2, got_2, cross, send_p, got_p,
    load_sem, halo_send, halo_recv, leg_send, leg_recv, one_send, one_recv,
    two_send, two_recv, p_send, p_recv,
):
    levels, _, _, _ = ext.shape
    rows, width = drow.shape
    tiles = width // LANES
    steps = leg.shape[1]
    waves = leg.shape[0] // rows
    n = n_lat * n_lev
    half = n_lat // 2
    group = waves // half
    rep = n_lev // group
    lv = levels // rep
    own = waves // n_lat
    l, e = lax.axis_index("lat"), lax.axis_index("lev")
    me = l * n_lev + e
    parity, lh = lax.div(l, half), lax.rem(l, half)
    share = lax.rem(e, rep)
    slot = group * lh + lax.div(e, rep)
    has_up, has_down = l > 0, l < n_lat - 1
    east, west = lax.rem(e + 1, n_lev), lax.rem(e + n_lev - 1, n_lev)

    def device(off):
        d = lax.rem(me + off, n)
        return lax.div(d, n_lev), lax.rem(d, n_lev)

    loads = []

    def load(src, dst):
        copy = pltpu.make_async_copy(src, dst, load_sem.at[len(loads)])
        copy.start()
        loads.append(copy)

    for t in range(tiles):
        load(
            field_hbm.at[:, :, pl.ds(t * LANES, LANES)],
            ext.at[:, t + 1, pl.ds(8, rows), :],
        )
    load(weights_hbm, wts)
    load(drow_hbm, drow)
    load(dcol_hbm, dcol)
    load(table_hbm.at[:, pl.ds(pl.multiple_of(e * width, LANES), width)], tab)
    load(leg_hbm, leg)

    barrier = pltpu.get_barrier_semaphore()

    @each(1, n)
    def _(off):
        lat, lev = device(off)
        pl.semaphore_signal(barrier, inc=1, device_id=(lat, lev), device_id_type=MESH)

    lane = lax.broadcasted_iota(jnp.int32, (rows, LANES), 1)
    for t in range(tiles):
        loads[t].wait()
    for v in range(levels):
        for t in range(tiles):
            cols = slice(t * LANES, (t + 1) * LANES)
            pack_row[0, 2 * v : 2 * v + 2, cols] = ext[v, t + 1, 6 + rows : 8 + rows, :]
            pack_row[1, 2 * v : 2 * v + 2, cols] = ext[v, t + 1, 8:10, :]
    last = jnp.zeros((rows, LANES), F32)
    first = jnp.zeros((rows, LANES), F32)
    for v in range(levels):
        here = (lane == 2 * v) | (lane == 2 * v + 1)
        tail = pltpu.roll(ext[v, tiles, 8 : 8 + rows, :], (2 * v + 2) % LANES, 1)
        last = jnp.where(here, tail, last)
        head = ext[v, 1, 8 : 8 + rows, :]
        if v:
            head = pltpu.roll(head, 2 * v, 1)
        first = jnp.where(here, head, first)
    pack_col[0] = last
    pack_col[1] = first

    def shift_block(v, t, row0, size, moves=(-2, -1, 1, 2)):
        at = pl.ds(row0, size)
        at_lane = lax.broadcasted_iota(jnp.int32, (size, LANES), 1)
        here = ext[v, t + 1, at, :]
        left = ext[v, t, at, :] if min(moves) < 0 else None
        right = ext[v, t + 2, at, :] if max(moves) > 0 else None
        for move in moves:
            n_move = (-2, -1, 1, 2).index(move)
            amount = (-move) % LANES
            mine = pltpu.roll(here, amount, 1)
            if move < 0:
                moved = jnp.where(at_lane < -move, pltpu.roll(left, amount, 1), mine)
            else:
                moved = jnp.where(at_lane >= LANES - move, pltpu.roll(right, amount, 1), mine)
            shifted[n_move, v, t, at, :] = moved

    def shift_inner(chosen):
        def step(t, carry):
            for v in chosen:
                shift_block(v, t, 8, rows)
            return carry

        lax.fori_loop(1, tiles - 1, step, 0)

    groups = rows // 8

    def advect(t, chosen):
        cols = pl.ds(pl.multiple_of(t * LANES, LANES), LANES)
        corner = [wts[ab, :, cols].astype(F32) for ab in range(4)]
        for g in chosen:
            band = slice(8 * g, 8 * g + 8)
            dr, dc = drow[band, cols], dcol[band, cols]
            zero = jnp.zeros((8, LANES), F32)
            in_col = {c: dc == c for c in range(-2, 2)}
            in_row = {r: dr == r for r in range(-2, 2)}

            def pick(masks, at, one, two):
                value = zero
                if at - 1 in masks:
                    value = jnp.where(masks[at - 1], two, value)
                if at in masks:
                    value = jnp.where(masks[at], one, value)
                return value

            part = [
                [pick(in_col, c, corner[2 * a][band], corner[2 * a + 1][band]) for c in range(-2, 3)]
                for a in range(2)
            ]
            coef = [
                [pick(in_row, r, part[0][c], part[1][c]) for c in range(5)] for r in range(-2, 3)
            ]
            for v in range(levels):
                total = None
                for r in range(5):
                    at = pl.ds(8 * g + 6 + r, 8)
                    for c in range(5):
                        if c == 2:
                            value = ext[v, t + 1, at, :]
                        else:
                            value = shifted[c if c < 2 else c - 1, v, t, at, :]
                        term = coef[r][c] * value
                        total = term if total is None else total + term
                adv[v * rows + 8 * g : v * rows + 8 * g + 8, cols] = total

    def advect_inner(t, carry):
        advect(t, range(1, groups - 1))
        return carry

    shift_inner(range(levels // 2))

    pl.semaphore_wait(barrier, n - 1)

    def remote(src, dst, ssem, rsem, lat, lev):
        return pltpu.make_async_remote_copy(
            src_ref=src, dst_ref=dst, send_sem=ssem, recv_sem=rsem,
            device_id=(lat, lev), device_id_type=MESH,
        )

    def halo(n, src, dst, lat, lev):
        return remote(src, dst, halo_send.at[n], halo_recv.at[n], lat, lev)

    bottom, top = pl.ds(rows - 8, 8), pl.ds(0, 8)
    flat = [
        halo(0, pack_col.at[0], got_col.at[0], l, east),
        halo(1, pack_col.at[1], got_col.at[1], l, west),
    ]
    below = [
        halo(2, pack_row.at[0], got_row.at[0], l + 1, e),
        halo(3, pack_col.at[0, bottom], got_corner.at[0], l + 1, east),
        halo(4, pack_col.at[1, bottom], got_corner.at[1], l + 1, west),
    ]
    above = [
        halo(5, pack_row.at[1], got_row.at[1], l - 1, e),
        halo(6, pack_col.at[0, top], got_corner.at[2], l - 1, east),
        halo(7, pack_col.at[1, top], got_corner.at[3], l - 1, west),
    ]

    @pl.when(has_down)
    def _():
        for copy in below:
            copy.start()

    @pl.when(has_up)
    def _():
        for copy in above:
            copy.start()

    for copy in flat:
        copy.start()

    first = lax.broadcasted_iota(jnp.int32, (1, 4 * waves), 1)
    slot_row = jnp.zeros((1, 4 * waves), jnp.int32)
    for k in range(waves):
        slot_row = jnp.where(lax.rem(first, waves) == k, slot_ref[k], slot_row)
    at = lambda shape, dim: lax.broadcasted_iota(jnp.int32, shape, dim)
    iota_f = (4 * waves, 4 * waves)
    order = one_hot(
        (lax.div(at(iota_f, 0), waves) == lax.div(at(iota_f, 1), waves))
        & (lax.rem(at(iota_f, 0), waves) == slot_row)
    )
    stage[...] = jnp.zeros_like(stage)
    cross[...] = jnp.zeros_like(cross)
    padded = send_leg.shape[1]
    basis[:, padded:, :] = jnp.zeros((half, HALF - padded, steps), BF16)

    shift_inner(range(levels // 2, levels))
    if tiles > 1:
        for v in range(levels):
            shift_block(v, 0, 8, rows, (1, 2))
            shift_block(v, tiles - 1, 8, rows, (-2, -1))
    for t in range(tiles, tiles + 3):
        loads[t].wait()
    lax.fori_loop(1, tiles - 1, advect_inner, 0)

    loads[tiles + 4].wait()
    send_leg[...] = jnp.zeros_like(send_leg)
    band = 8
    iota_g = (half * band, band * waves)
    slot_cols = jnp.zeros((1, band * waves), jnp.int32)
    lane_k = lax.rem(lax.broadcasted_iota(jnp.int32, (1, band * waves), 1), waves)
    for k in range(waves):
        slot_cols = jnp.where(lane_k == k, slot_ref[k], slot_cols)
    choose = one_hot(
        (lax.rem(at(iota_g, 0), band) == lax.div(at(iota_g, 1), waves))
        & (group * lax.div(at(iota_g, 0), band) + lax.div(e, rep) == slot_cols)
    )
    for i in range(0, rows, band):
        picked = jnp.dot(
            choose, leg[i * waves : (i + band) * waves, :], preferred_element_type=F32
        ).astype(BF16)
        for t in range(half):
            send_leg[t, i : i + band, :] = picked[t * band : (t + 1) * band]
    slots_of = lambda t: basis.at[t, pl.ds(0, padded), :]
    copies_g = []
    for off in range(1, half):
        t = lax.rem(lh + off, half)
        copy = remote(
            send_leg.at[t], slots_of(lh), leg_send.at[off], leg_recv.at[lh],
            parity * half + t, e,
        )
        copy.start()
        copies_g.append(copy)
    basis[lh, 0:padded, :] = send_leg[lh]

    loads[tiles + 3].wait()
    tabs[...] = jnp.dot(order, tab[...], preferred_element_type=F32).astype(BF16)


    def spread(piece, v):
        return pltpu.roll(piece, LANES - 2 - 2 * v, 1)

    def spread_east(piece, v):
        return pltpu.roll(piece, LANES - 2 * v, 1) if v else piece

    def rim(row0, size, from_west, from_east):
        for v in range(levels):
            ext[v, 0, row0 : row0 + size, :] = spread(from_west, v)
            ext[v, tiles + 1, row0 : row0 + size, :] = spread_east(from_east, v)

    def fill_rows(which, row0):
        for v in range(levels):
            for t in range(tiles):
                cols = slice(t * LANES, (t + 1) * LANES)
                ext[v, t + 1, row0 : row0 + 2, :] = got_row[which, 2 * v : 2 * v + 2, cols]

    @pl.when(has_up)
    def _():
        for copy in below:
            copy.wait_recv()
        fill_rows(0, 6)
        rim(0, 8, got_corner[0], got_corner[1])

    @pl.when(jnp.logical_not(has_up))
    def _():
        ext[:, :, 0:8, :] = jnp.zeros((levels, tiles + 2, 8, LANES), F32)

    @pl.when(has_down)
    def _():
        for copy in above:
            copy.wait_recv()
        fill_rows(1, rows + 8)
        rim(rows + 8, 8, got_corner[2], got_corner[3])

    @pl.when(jnp.logical_not(has_down))
    def _():
        ext[:, :, rows + 8 : rows + 16, :] = jnp.zeros((levels, tiles + 2, 8, LANES), F32)

    for copy in flat:
        copy.wait_recv()
    rim(8, rows, got_col[0], got_col[1])

    def shift_rims(t, carry):
        for v in range(levels):
            shift_block(v, t, 0, 8)
            shift_block(v, t, rows + 8, 8)
        return carry

    edges = min(tiles, 2)
    for v in range(levels):
        shift_block(v, 0, 8, rows, (-2, -1))
        shift_block(v, tiles - 1, 8, rows, (1, 2))
    lax.fori_loop(0, tiles, shift_rims, 0)
    outer = sorted({0, groups - 1})

    def advect_rims(t, carry):
        advect(t, outer)
        return carry

    def advect_edge(n, carry):
        advect(n * (tiles - 1), range(groups))
        return carry

    lax.fori_loop(0, edges, advect_edge, 0)
    lax.fori_loop(1, tiles - 1, advect_rims, 0)

    contract_last = (((1,), (1,)), ((), ()))
    for v in range(levels):
        value = adv[v * rows : (v + 1) * rows, :]
        lead = value.astype(BF16)
        rest = (value - lead.astype(F32)).astype(BF16)
        both = lax.dot_general(tabs[...], lead, contract_last, preferred_element_type=F32)
        more = lax.dot_general(
            tabs[0 : 2 * waves, :], rest, contract_last, preferred_element_type=F32
        )
        coeffs = both[0 : 2 * waves] + both[2 * waves :] + more
        stage[v * waves : (v + 1) * waves, 0:rows] = coeffs[0:waves]
        stage[v * waves : (v + 1) * waves, HALF : HALF + rows] = coeffs[waves:]
    owners = half * n_lev
    for s in range(waves):
        for g in range(rep):
            send_1[s * rep + g] = stage[pl.ds(g * lv * waves + s, lv, stride=waves), :]

    def copy_1(off):
        lat, lev = device(off)
        owner = lax.rem(lat, half) * n_lev + lev
        return remote(
            send_1.at[owner], got_1.at[me], one_send.at[off], one_recv.at[me], lat, lev
        )

    @each(1, n)
    def _(off):
        copy_1(off).start()

    got_1[me] = send_1[lh * n_lev + e]

    spread_rows = 2 * waves * levels
    iota_w = (spread_rows, 2 * waves)
    repeat = one_hot(lax.div(at(iota_w, 0), levels) == at(iota_w, 1))
    for q in range(2):
        wide[q] = jnp.dot(
            repeat, tabs[2 * waves * q : 2 * waves * (q + 1), :], preferred_element_type=F32
        ).astype(BF16)

    at_row, at_col = at((LANES, LANES), 0), at((LANES, LANES), 1)
    flip = one_hot(
        ((at_row + at_col == rows - 1) & (at_row < HALF) & (at_col < HALF))
        | ((at_row + at_col == 2 * HALF + rows - 1) & (at_row >= HALF) & (at_col >= HALF))
    )
    sign = jnp.where(parity == 0, 1.0, -1.0).astype(F32)
    iota_e = (rows, 4 * LANES)
    row_e, col_e = at(iota_e, 0), at(iota_e, 1)
    part_e, lane_e = lax.div(col_e, LANES), lax.rem(col_e, LANES)
    place = HALF * lax.div(part_e, 2)
    natural = (lax.rem(part_e, 2) == 1) & (lane_e == row_e + place)
    turned = (lax.rem(part_e, 2) == 0) & (lane_e == rows - 1 - row_e + place)
    gather = (jnp.where(natural, sign, 0.0) + jnp.where(turned, 1.0, 0.0)).astype(BF16)

    wave_own = jnp.int32(0)
    for k in range(waves):
        wave_own = jnp.where(slot_ref[k] == slot, k, wave_own)
    wave_own = wave_own * (NT + 1) // waves
    column = lax.broadcasted_iota(jnp.int32, (2 * lv, steps), 1)
    degree = wave_own + 2 * column + parity
    factor = 1.0 / (
        1.0 + DAMPING * (degree * (degree + 1)).astype(F32) / float(NT * (NT + 1))
    )
    forward_scale = 1.0 / math.sqrt(rows * n_lat // 2)
    inverse_scale = math.sqrt(NLON) / math.sqrt(waves) / math.sqrt(steps)
    scale = jnp.where(wave_own == 0, inverse_scale, 2.0 * inverse_scale).astype(F32)

    for off in range(1, half):
        t = lax.rem(lh + off, half)
        remote(
            send_leg.at[t], slots_of(t), leg_send.at[off], leg_recv.at[t], parity * half + t, e
        ).wait_recv()

    def wait_1(off):
        lat, lev = device(off)
        d = lat * n_lev + lev
        remote(send_1.at[0], got_1.at[d], one_send.at[off], one_recv.at[d], lat, lev).wait_recv()

    @each(1, n)
    def _(off):
        wait_1(off)

    low = lax.broadcasted_iota(jnp.int32, (lv, LANES), 1) < HALF

    def total_1(lat):
        value = got_1[lat * n_lev]
        for d in range(1, n_lev):
            value = value + got_1[lat * n_lev + d]
        return value

    for b in range(0, half, 2):
        cols = slice(b * HALF, b * HALF + LANES)
        for which in range(2):
            lat = parity * half + b
            one = total_1(lat if which == 0 else n_lat - 1 - lat)
            two = total_1(lat + 1 if which == 0 else n_lat - 2 - lat)
            row0 = which * 2 * lv
            both_f[row0 : row0 + lv, cols] = jnp.where(low, one, pltpu.roll(two, HALF, 1))
            both_f[row0 + lv : row0 + 2 * lv, cols] = jnp.where(
                low, pltpu.roll(one, HALF, 1), two
            )
    near = both_f[0 : 2 * lv, :].astype(BF16)
    both_b[0 : 2 * lv, :] = near
    for c0 in range(0, half * HALF, LANES):
        cols = slice(c0, c0 + LANES)
        both_b[2 * lv :, cols] = jnp.dot(
            both_f[2 * lv :, cols].astype(BF16), flip, preferred_element_type=F32
        ).astype(BF16)
    matrix = basis[...].reshape(half * HALF, steps)
    raw = jnp.dot(both_b[...], matrix, preferred_element_type=F32)
    raw = (raw[2 * lv :] + sign * raw[0 : 2 * lv]) * forward_scale
    masked = jnp.where(degree <= NT, raw, 0.0)
    damped = masked * factor
    change = (damped - masked).astype(BF16)
    back = lax.dot_general(change, matrix, contract_last, preferred_element_type=F32) * scale
    both_f[0 : 2 * lv, :] = back
    for b in range(0, half, 2):
        cols = slice(b * HALF, b * HALF + LANES)
        real, imag = both_f[0:lv, cols], both_f[lv : 2 * lv, cols]
        send_2[b] = jnp.where(low, real, pltpu.roll(imag, HALF, 1))
        send_2[b + 1] = jnp.where(low, pltpu.roll(real, HALF, 1), imag)

    def copy_2(off):
        lat, lev = device(off)
        inside = lax.div(lat, half) == parity
        block = jnp.where(inside, lat, n_lat - 1 - lat) - parity * half
        return remote(
            send_2.at[block], got_2.at[me], two_send.at[off], two_recv.at[me], lat, lev
        )

    @each(1, n)
    def _(off):
        copy_2(off).start()

    got_2[me] = send_2[lh]

    for vv in range(lv):
        for c in range(2):
            send_p[vv, c : c + 1, :] = damped[c * lv + vv : c * lv + vv + 1]
    home, place_p = lax.div(slot, own), lax.rem(slot, own)
    for vv in range(lv):
        lev = share * lv + vv
        mine = (home == l) & (lev == e)
        copy = remote(
            send_p.at[vv], got_p.at[place_p, parity], p_send.at[vv],
            p_recv.at[place_p, parity], home, lev,
        )
        pl.when(jnp.logical_not(mine))(copy.start)

        @pl.when(mine)
        def _():
            got_p[place_p, parity] = send_p[vv]

    def wait_2(off):
        lat, lev = device(off)
        d = lat * n_lev + lev
        remote(send_2.at[0], got_2.at[d], two_send.at[off], two_recv.at[d], lat, lev).wait_recv()

    @each(1, n)
    def _(off):
        wait_2(off)

    pairs = waves * levels
    for which in range(2):
        start = jnp.where(which == 1, parity, 1 - parity) * owners
        for o in range(owners):
            stage[which * pairs + o * lv : which * pairs + (o + 1) * lv, :] = got_2[start + o]
    for which in range(2):
        value = stage[which * pairs : (which + 1) * pairs, :]
        lead = value.astype(BF16)
        rest = (value - lead.astype(F32)).astype(BF16)
        for c in range(2):
            cols = slice((2 * c + which) * LANES, (2 * c + which + 1) * LANES)
            cross[0, c * pairs : (c + 1) * pairs, cols] = lead
            cross[1, c * pairs : (c + 1) * pairs, cols] = rest
    synth[...] = lax.dot_general(
        gather, cross[0], contract_last, preferred_element_type=F32
    ) + lax.dot_general(gather, cross[1], contract_last, preferred_element_type=F32)

    for so in range(own):
        for pp in range(2):
            from_slot = own * l + so
            lat = pp * half + lax.div(from_slot, group)
            lev = lax.rem(from_slot, group) * rep + lax.div(e, lv)
            copy = remote(
                send_p.at[0], got_p.at[so, pp], p_send.at[0], p_recv.at[so, pp], lat, lev
            )
            pl.when(jnp.logical_not((lat == l) & (lev == e)))(copy.wait_recv)
    spec_ref[...] = got_p[...]

    for copy in flat + copies_g:
        copy.wait_send()

    @each(1, n)
    def _(off):
        copy_1(off).wait_send()
        copy_2(off).wait_send()

    for vv in range(lv):
        lev = share * lv + vv
        copy = remote(
            send_p.at[vv], got_p.at[place_p, parity], p_send.at[vv],
            p_recv.at[place_p, parity], home, lev,
        )
        pl.when(jnp.logical_not((home == l) & (lev == e)))(copy.wait_send)

    @pl.when(has_down)
    def _():
        for copy in below:
            copy.wait_send()

    @pl.when(has_up)
    def _():
        for copy in above:
            copy.wait_send()


def finish(adv, synth, wide, spec, out_hbm, spec_hbm, lead_all, rest_all, result, sems):
    levels, rows, width = result.shape
    spec_copy = pltpu.make_async_copy(spec, spec_hbm, sems.at[0])
    spec_copy.start()
    value = synth[...]
    lead = value.astype(BF16).astype(F32)
    rest = value - lead
    level_of = lax.rem(lax.broadcasted_iota(jnp.int32, value.shape, 1), levels)
    for v in range(levels):
        at = slice(v * rows, (v + 1) * rows)
        lead_all[at, :] = jnp.where(level_of == v, lead, 0.0).astype(BF16)
        rest_all[at, :] = jnp.where(level_of == v, rest, 0.0).astype(BF16)
    chunk = min(width, 256)
    copies = []
    for j in range(0, width, chunk):
        cols = slice(j, j + chunk)
        increment = (
            jnp.dot(lead_all[...], wide[0, :, cols], preferred_element_type=F32)
            + jnp.dot(lead_all[...], wide[1, :, cols], preferred_element_type=F32)
            + jnp.dot(rest_all[...], wide[0, :, cols], preferred_element_type=F32)
        )
        updated = adv[:, cols] + increment
        for v in range(levels):
            result[v, :, cols] = updated[v * rows : (v + 1) * rows]
        copy = pltpu.make_async_copy(
            result.at[:, :, cols], out_hbm.at[:, :, cols], sems.at[1 + j // chunk]
        )
        copy.start()
        copies.append(copy)
    for copy in copies + [spec_copy]:
        copy.wait()


def solution(mesh):
    n_lat, n_lev = mesh.shape["lat"], mesh.shape["lev"]

    def on_device(field, weights, depart_row, depart_col, legendre, wave_slot):
        levels, rows, width = field.shape
        _, waves, steps = legendre.shape
        tiles = width // LANES
        own = waves // n_lat
        n, half = n_lat * n_lev, n_lat // 2
        owners = half * n_lev
        rep = n_lev // (waves // half)
        lv = levels // rep
        pairs = waves * levels
        table = jnp.asarray(lon_table(waves))
        vmem, dma = pltpu.VMEM, pltpu.SemaphoreType.DMA
        anywhere = pl.BlockSpec(memory_space=pltpu.HBM)
        in_vmem = pl.BlockSpec(memory_space=pltpu.VMEM)
        adv, synth, wide, spec = pl.pallas_call(
            functools.partial(kernel, n_lat, n_lev),
            out_shape=(
                vmem((levels * rows, width), F32),
                vmem((rows, 2 * pairs), F32),
                vmem((2, 2 * pairs, width), BF16),
                vmem((own, 2, 2, steps), F32),
            ),
            in_specs=[pl.BlockSpec(memory_space=pltpu.SMEM)] + [anywhere] * 6,
            out_specs=(in_vmem,) * 4,
            scratch_shapes=[
                vmem((levels, tiles + 2, rows + 16, LANES), F32),
                vmem((4, levels, tiles, rows + 16, LANES), F32),
                vmem((4, rows, width), BF16),
                vmem((rows, width), jnp.int32),
                vmem((rows, width), jnp.int32),
                vmem((rows * waves, steps), BF16),
                vmem((4 * waves, width), BF16),
                vmem((4 * waves, width), BF16),
                vmem((2, 2 * levels, width), F32),
                vmem((2, rows, LANES), F32),
                vmem((2, 2 * levels, width), F32),
                vmem((2, rows, LANES), F32),
                vmem((4, 8, LANES), F32),
                vmem((half, -(-rows // 16) * 16, steps), BF16),
                vmem((half, HALF, steps), BF16),
                vmem((2 * pairs, LANES), F32),
                vmem((owners, lv, LANES), F32),
                vmem((n, lv, LANES), F32),
                vmem((4 * lv, half * HALF), F32),
                vmem((4 * lv, half * HALF), BF16),
                vmem((half, lv, LANES), F32),
                vmem((n, lv, LANES), F32),
                vmem((2, 2 * pairs, 4 * LANES), BF16),
                vmem((lv, 2, steps), F32),
                vmem((own, 2, 2, steps), F32),
                dma((tiles + 5,)),
                dma((8,)), dma((8,)),
                dma((half,)), dma((half,)),
                dma((n,)), dma((n,)),
                dma((n,)), dma((n,)),
                dma((lv,)), dma((own, 2)),
            ],
            compiler_params=pltpu.CompilerParams(
                collective_id=0, has_side_effects=True, vmem_limit_bytes=40 << 20
            ),
        )(
            wave_slot,
            *(
                pltpu.with_memory_space_constraint(x, pltpu.HBM)
                for x in (
                    field, weights, depart_row, depart_col,
                    legendre.reshape(rows * waves, steps), table,
                )
            ),
        )
        chunks = width // min(width, 256)
        updated, spectral = pl.pallas_call(
            finish,
            out_shape=(
                jax.ShapeDtypeStruct((levels, rows, width), F32),
                jax.ShapeDtypeStruct((own, 2, 2, steps), F32),
            ),
            in_specs=[in_vmem] * 4,
            out_specs=(anywhere,) * 2,
            scratch_shapes=[
                vmem((levels * rows, 2 * pairs), BF16),
                vmem((levels * rows, 2 * pairs), BF16),
                vmem((levels, rows, width), F32),
                dma((1 + chunks,)),
            ],
            compiler_params=pltpu.CompilerParams(vmem_limit_bytes=20 << 20),
        )(*(pltpu.with_memory_space_constraint(x, vmem) for x in (adv, synth, wide, spec)))
        return updated, spectral.reshape(own, 2, 1, 2, steps)

    placed = (
        P(None, "lat", "lev"),
        P(None, "lat", "lev"),
        P("lat", "lev"),
        P("lat", "lev"),
        P("lat", None, None),
        P(),
    )
    return jax.shard_map(
        on_device,
        mesh=mesh,
        in_specs=placed,
        out_specs=(P(None, "lat", "lev"), P("lat", None, "lev", None, None)),
        check_vma=False,
    )
```

time: 39.8 us -> 28.4 us (0.71)
  Pallas kernels: 36.4 us -> 26.9 us
  local copies, waits for them, and re-layouts: 2.6 us -> 0.65 us
    pallas_call x1 -> x2, Pallas kernels: 36.4 us -> 26.9 us  [the longest x1 25.8 us: on_device(): pl.pallas_call(functools.partial(kernel, n_lat, n_lev), out_shape=(vmem((...]
    unnamed x4 -> x2, local copies, waits for them, and re-layouts: 2.6 us -> 0.65 us
where the time goes in v1:
time: 28.4 us; the launch traced here: 28.2 us
  Pallas kernels  26.9 us (95%)
  local copies, waits for them, and re-layouts  0.65 us (2%)
  between operations  0.65 us (2%)
    pallas_call x1, Pallas kernels, on_device(): pl.pallas_call(functools.partial(kernel, n_lat, n_lev), out_shape=(vmem((...  25.8 us
    pallas_call x1, Pallas kernels, on_device(): pl.pallas_call(finish, out_shape=(jax.ShapeDtypeStruct((levels, rows, wid...  1.18 us
    unnamed x2, local copies, waits for them, and re-layouts  0.65 us

profile of v1, /device:TPU:0, one launch (start us, length us, event | category | flops | bytes accessed | tf_op | source)
XLA Modules:
  0.0 28.2 jit_solution(18044882802009464285)
XLA Ops:
  0.6 0.0 copy-start
  0.6 0.6 %copy-done = s32[16]{0:T(128)S(1)} copy-done((s32[16]{0:T(128)S(1)}, s32[16]{0:T(128)}, u32[]{:S(2)}) %copy-start) | copy-done | bytes 88
  1.3 25.8 %shard_map.86 = (f32[160,1024]{1,0:T(8,128)S(1)}, f32[40,128]{1,0:T(8,128)S(1)}, bf16[2,128,1024]{2,1,0:T(8,128)(2,1)S(1)}, f32[2,2,2,640]{3,2,1,0:T(2,128)S(1)}) custom-call(s32[16]{0:T(128)S(1)} %copy-done, f32[4,40,1024]{2,1,0:T(8,128)} %field_hbm.1, bf16[4,40,1024]{2,1,0:T(8,128)(2,1)} %weights_hbm.1, s32[40,1024]{1,0:T(8,128)} %drow_hbm.1, ...), custom_call_target="tpu_custom_call" | custom-call | tf_op jit(solution)/shard_map/pallas_call | solution.py:627
  27.1 1.2 %shard_map.87 = (f32[4,40,1024]{2,1,0:T(8,128)}, f32[2,2,2,640]{3,2,1,0:T(2,128)}) custom-call(f32[160,1024]{1,0:T(8,128)S(1)} %get-tuple-element.8.adv, f32[40,128]{1,0:T(8,128)S(1)} %get-tuple-element.9.synth, bf16[2,128,1024]{2,1,0:T(8,128)(2,1)S(1)} %get-tuple-element.10.wide, f32[2,2,2,640]{3,2,1,0:T(2,128)S(1)} %get-tuple-element.11.spec), custom_call_target="tpu_custom_call" | custom-call | tf_op jit(solution)/shard_map/pallas_call | solution.py:684
Async XLA Ops:
  0.6 0.7 %copy-start = (s32[16]{0:T(128)S(1)}, s32[16]{0:T(128)}, u32[]{:S(2)}) copy-start(s32[16]{0:T(128)} %slot_ref.1) | copy-start | bytes 196

commit v2 on v1

--- a/solution.py
+++ b/solution.py
@@ -47,9 +47,9 @@
 
 def kernel(
     n_lat, n_lev,
-    slot_ref, field_hbm, weights_hbm, drow_hbm, dcol_hbm, leg_hbm, table_hbm,
+    slot_hbm, field_hbm, weights_hbm, drow_hbm, dcol_hbm, leg_hbm, table_hbm,
     adv, synth, wide, spec_ref,
-    ext, shifted, wts, drow, dcol, leg, tab, tabs,
+    slot_ref, ext, shifted, wts, drow, dcol, leg, tab, tabs,
     pack_row, pack_col, got_row, got_col, got_corner,
     send_leg, basis, stage, send_1, got_1, both_f, both_b, send_2, got_2, cross, send_p, got_p,
     load_sem, halo_send, halo_recv, leg_send, leg_recv, one_send, one_recv,
@@ -95,6 +95,7 @@
     load(dcol_hbm, dcol)
     load(table_hbm.at[:, pl.ds(pl.multiple_of(e * width, LANES), width)], tab)
     load(leg_hbm, leg)
+    load(slot_hbm, slot_ref)
 
     barrier = pltpu.get_barrier_semaphore()
 
@@ -192,8 +193,6 @@
         advect(t, range(1, groups - 1))
         return carry
 
-    shift_inner(range(levels // 2))
-
     pl.semaphore_wait(barrier, n - 1)
 
     def remote(src, dst, ssem, rsem, lat, lev):
@@ -234,6 +233,7 @@
     for copy in flat:
         copy.start()
 
+    loads[tiles + 5].wait()
     first = lax.broadcasted_iota(jnp.int32, (1, 4 * waves), 1)
     slot_row = jnp.zeros((1, 4 * waves), jnp.int32)
     for k in range(waves):
@@ -249,7 +249,7 @@
     padded = send_leg.shape[1]
     basis[:, padded:, :] = jnp.zeros((half, HALF - padded, steps), BF16)
 
-    shift_inner(range(levels // 2, levels))
+    shift_inner(range(levels))
     if tiles > 1:
         for v in range(levels):
             shift_block(v, 0, 8, rows, (1, 2))
@@ -281,7 +281,7 @@
     for off in range(1, half):
         t = lax.rem(lh + off, half)
         copy = remote(
-            send_leg.at[t], slots_of(lh), leg_send.at[off], leg_recv.at[lh],
+            send_leg.at[t], slots_of(lh), leg_send, leg_recv,
             parity * half + t, e,
         )
         copy.start()
@@ -380,7 +380,7 @@
         lat, lev = device(off)
         owner = lax.rem(lat, half) * n_lev + lev
         return remote(
-            send_1.at[owner], got_1.at[me], one_send.at[off], one_recv.at[me], lat, lev
+            send_1.at[owner], got_1.at[me], one_send, one_recv, lat, lev
         )
 
     @each(1, n)
@@ -424,20 +424,13 @@
     inverse_scale = math.sqrt(NLON) / math.sqrt(waves) / math.sqrt(steps)
     scale = jnp.where(wave_own == 0, inverse_scale, 2.0 * inverse_scale).astype(F32)
 
-    for off in range(1, half):
-        t = lax.rem(lh + off, half)
-        remote(
-            send_leg.at[t], slots_of(t), leg_send.at[off], leg_recv.at[t], parity * half + t, e
-        ).wait_recv()
-
-    def wait_1(off):
-        lat, lev = device(off)
-        d = lat * n_lev + lev
-        remote(send_1.at[0], got_1.at[d], one_send.at[off], one_recv.at[d], lat, lev).wait_recv()
-
-    @each(1, n)
-    def _(off):
-        wait_1(off)
+    legs = send_leg.at[pl.ds(0, half - 1)]
+    pltpu.make_async_copy(legs, legs, leg_recv).wait()
+
+    def all_of(ref, sem, count=n - 1):
+        return pltpu.make_async_copy(ref.at[pl.ds(0, count)], ref.at[pl.ds(0, count)], sem)
+
+    all_of(got_1, one_recv).wait()
 
     low = lax.broadcasted_iota(jnp.int32, (lv, LANES), 1) < HALF
 
@@ -484,7 +477,7 @@
         inside = lax.div(lat, half) == parity
         block = jnp.where(inside, lat, n_lat - 1 - lat) - parity * half
         return remote(
-            send_2.at[block], got_2.at[me], two_send.at[off], two_recv.at[me], lat, lev
+            send_2.at[block], got_2.at[me], two_send, two_recv, lat, lev
         )
 
     @each(1, n)
@@ -501,23 +494,15 @@
         lev = share * lv + vv
         mine = (home == l) & (lev == e)
         copy = remote(
-            send_p.at[vv], got_p.at[place_p, parity], p_send.at[vv],
-            p_recv.at[place_p, parity], home, lev,
+            send_p.at[vv], got_p.at[2 * place_p + parity], p_send, p_recv, home, lev
         )
         pl.when(jnp.logical_not(mine))(copy.start)
 
         @pl.when(mine)
         def _():
-            got_p[place_p, parity] = send_p[vv]
-
-    def wait_2(off):
-        lat, lev = device(off)
-        d = lat * n_lev + lev
-        remote(send_2.at[0], got_2.at[d], two_send.at[off], two_recv.at[d], lat, lev).wait_recv()
-
-    @each(1, n)
-    def _(off):
-        wait_2(off)
+            got_p[2 * place_p + parity] = send_p[vv]
+
+    all_of(got_2, two_recv).wait()
 
     pairs = waves * levels
     for which in range(2):
@@ -536,32 +521,23 @@
         gather, cross[0], contract_last, preferred_element_type=F32
     ) + lax.dot_general(gather, cross[1], contract_last, preferred_element_type=F32)
 
-    for so in range(own):
-        for pp in range(2):
-            from_slot = own * l + so
-            lat = pp * half + lax.div(from_slot, group)
-            lev = lax.rem(from_slot, group) * rep + lax.div(e, lv)
-            copy = remote(
-                send_p.at[0], got_p.at[so, pp], p_send.at[0], p_recv.at[so, pp], lat, lev
-            )
-            pl.when(jnp.logical_not((lat == l) & (lev == e)))(copy.wait_recv)
-    spec_ref[...] = got_p[...]
-
-    for copy in flat + copies_g:
+    keeps = (home == l) & (share == lax.div(e, lv))
+    spec_waits = [
+        (keeps, all_of(got_p, p_recv, 2 * own - 1)),
+        (jnp.logical_not(keeps), all_of(got_p, p_recv, 2 * own)),
+    ]
+    for case, copy in spec_waits:
+        pl.when(case)(copy.wait)
+    for k in range(2 * own):
+        spec_ref[k] = got_p[k]
+
+    for copy in flat:
         copy.wait_send()
-
-    @each(1, n)
-    def _(off):
-        copy_1(off).wait_send()
-        copy_2(off).wait_send()
-
-    for vv in range(lv):
-        lev = share * lv + vv
-        copy = remote(
-            send_p.at[vv], got_p.at[place_p, parity], p_send.at[vv],
-            p_recv.at[place_p, parity], home, lev,
-        )
-        pl.when(jnp.logical_not((home == l) & (lev == e)))(copy.wait_send)
+    pltpu.make_async_copy(legs, legs, leg_send).wait()
+    all_of(got_1, one_send).wait()
+    all_of(got_2, two_send).wait()
+    pl.when(keeps)(all_of(send_p, p_send, lv - 1).wait)
+    pl.when(jnp.logical_not(keeps))(all_of(send_p, p_send, lv).wait)
 
     @pl.when(has_down)
     def _():
@@ -630,11 +606,12 @@
                 vmem((levels * rows, width), F32),
                 vmem((rows, 2 * pairs), F32),
                 vmem((2, 2 * pairs, width), BF16),
-                vmem((own, 2, 2, steps), F32),
+                vmem((2 * own, 2, steps), F32),
             ),
-            in_specs=[pl.BlockSpec(memory_space=pltpu.SMEM)] + [anywhere] * 6,
+            in_specs=[anywhere] * 7,
             out_specs=(in_vmem,) * 4,
             scratch_shapes=[
+                pltpu.SMEM((waves,), jnp.int32),
                 vmem((levels, tiles + 2, rows + 16, LANES), F32),
                 vmem((4, levels, tiles, rows + 16, LANES), F32),
                 vmem((4, rows, width), BF16),
@@ -659,23 +636,22 @@
                 vmem((n, lv, LANES), F32),
                 vmem((2, 2 * pairs, 4 * LANES), BF16),
                 vmem((lv, 2, steps), F32),
-                vmem((own, 2, 2, steps), F32),
-                dma((tiles + 5,)),
+                vmem((2 * own, 2, steps), F32),
+                dma((tiles + 6,)),
                 dma((8,)), dma((8,)),
-                dma((half,)), dma((half,)),
-                dma((n,)), dma((n,)),
-                dma((n,)), dma((n,)),
-                dma((lv,)), dma((own, 2)),
+                dma, dma,
+                dma, dma,
+                dma, dma,
+                dma, dma,
             ],
             compiler_params=pltpu.CompilerParams(
                 collective_id=0, has_side_effects=True, vmem_limit_bytes=40 << 20
             ),
         )(
-            wave_slot,
             *(
                 pltpu.with_memory_space_constraint(x, pltpu.HBM)
                 for x in (
-                    field, weights, depart_row, depart_col,
+                    wave_slot, field, weights, depart_row, depart_col,
                     legendre.reshape(rows * waves, steps), table,
                 )
             ),
@@ -685,7 +661,7 @@
             finish,
             out_shape=(
                 jax.ShapeDtypeStruct((levels, rows, width), F32),
-                jax.ShapeDtypeStruct((own, 2, 2, steps), F32),
+                jax.ShapeDtypeStruct((2 * own, 2, steps), F32),
             ),
             in_specs=[in_vmem] * 4,
             out_specs=(anywhere,) * 2,

time: 28.4 us -> 25.8 us (0.908)
  Pallas kernels: 26.9 us -> 25 us
  local copies, waits for them, and re-layouts: 0.65 us -> 0 us
    pallas_call x1, Pallas kernels: 25.8 us -> 23.9 us  [on_device(): pl.pallas_call(functools.partial(kernel, n_lat, n_lev), out_shape=(vmem((...]
    unnamed x2 -> x0, local copies, waits for them, and re-layouts: 0.65 us -> none
where the time goes in v2:
time: 25.8 us; the launch traced here: 25.7 us
  Pallas kernels  25 us (97%)
  between operations  0.64 us (2%)
    pallas_call x1, Pallas kernels, on_device(): pl.pallas_call(functools.partial(kernel, n_lat, n_lev), out_shape=(vmem((...  23.9 us
    pallas_call x1, Pallas kernels, on_device(): pl.pallas_call(finish, out_shape=(jax.ShapeDtypeStruct((levels, rows, wid...  1.17 us

profile of v2, /device:TPU:0, one launch (start us, length us, event | category | flops | bytes accessed | tf_op | source)
XLA Modules:
  0.0 25.7 jit_solution(12372668016693501805)
XLA Ops:
  0.6 23.9 %shard_map.86 = (f32[160,1024]{1,0:T(8,128)S(1)}, f32[40,128]{1,0:T(8,128)S(1)}, bf16[2,128,1024]{2,1,0:T(8,128)(2,1)S(1)}, f32[4,2,640]{2,1,0:T(2,128)S(1)}) custom-call(s32[16]{0:T(128)} %slot_hbm.1, f32[4,40,1024]{2,1,0:T(8,128)} %field_hbm.1, bf16[4,40,1024]{2,1,0:T(8,128)(2,1)} %weights_hbm.1, s32[40,1024]{1,0:T(8,128)} %drow_hbm.1, ...), custom_call_target="tpu_custom_call" | custom-call | tf_op jit(solution)/shard_map/pallas_call | solution.py:603
  24.5 1.2 %shard_map.87 = (f32[4,40,1024]{2,1,0:T(8,128)}, f32[4,2,640]{2,1,0:T(2,128)}) custom-call(f32[160,1024]{1,0:T(8,128)S(1)} %get-tuple-element.8.adv, f32[40,128]{1,0:T(8,128)S(1)} %get-tuple-element.9.synth, bf16[2,128,1024]{2,1,0:T(8,128)(2,1)S(1)} %get-tuple-element.10.wide, f32[4,2,640]{2,1,0:T(2,128)S(1)} %get-tuple-element.11.spec), custom_call_target="tpu_custom_call" | custom-call | tf_op jit(solution)/shard_map/pallas_call | solution.py:660

commit v3 on v2

--- a/solution.py
+++ b/solution.py
@@ -49,8 +49,8 @@
     n_lat, n_lev,
     slot_hbm, field_hbm, weights_hbm, drow_hbm, dcol_hbm, leg_hbm, table_hbm,
     adv, synth, wide, spec_ref,
-    slot_ref, ext, shifted, wts, drow, dcol, leg, tab, tabs,
-    pack_row, pack_col, got_row, got_col, got_corner,
+    slot_ref, ext, shifted, points, drow, dcol, leg, tab, tabs,
+    pack_row, pack_col, got_rim, got_col, rim_points, side_points, side,
     send_leg, basis, stage, send_1, got_1, both_f, both_b, send_2, got_2, cross, send_p, got_p,
     load_sem, halo_send, halo_recv, leg_send, leg_recv, one_send, one_recv,
     two_send, two_recv, p_send, p_recv,
@@ -78,24 +78,21 @@
         d = lax.rem(me + off, n)
         return lax.div(d, n_lev), lax.rem(d, n_lev)
 
-    loads = []
-
-    def load(src, dst):
-        copy = pltpu.make_async_copy(src, dst, load_sem.at[len(loads)])
+    def load(k, src, dst):
+        copy = pltpu.make_async_copy(src, dst, load_sem.at[k])
         copy.start()
-        loads.append(copy)
+        return copy
 
     for t in range(tiles):
-        load(
-            field_hbm.at[:, :, pl.ds(t * LANES, LANES)],
-            ext.at[:, t + 1, pl.ds(8, rows), :],
-        )
-    load(weights_hbm, wts)
-    load(drow_hbm, drow)
-    load(dcol_hbm, dcol)
-    load(table_hbm.at[:, pl.ds(pl.multiple_of(e * width, LANES), width)], tab)
-    load(leg_hbm, leg)
-    load(slot_hbm, slot_ref)
+        load(0, field_hbm.at[:, :, pl.ds(t * LANES, LANES)], ext.at[:, t, pl.ds(8, rows), :])
+    load_leg = load(1, leg_hbm, leg)
+    load_slot = load(2, slot_hbm, slot_ref)
+    load_wts = load(3, weights_hbm, points.at[pl.ds(0, 4 * rows), :])
+    load_row = load(4, drow_hbm, drow)
+    load_col = load(5, dcol_hbm, dcol)
+    load_tab = load(
+        6, table_hbm.at[:, pl.ds(pl.multiple_of(e * width, LANES), width)], tab
+    )
 
     barrier = pltpu.get_barrier_semaphore()
 
@@ -104,96 +101,35 @@
         lat, lev = device(off)
         pl.semaphore_signal(barrier, inc=1, device_id=(lat, lev), device_id_type=MESH)
 
-    lane = lax.broadcasted_iota(jnp.int32, (rows, LANES), 1)
-    for t in range(tiles):
-        loads[t].wait()
+    at = lambda shape, dim: lax.broadcasted_iota(jnp.int32, shape, dim)
+    for row0 in (0, rows + 8):
+        zero = jnp.zeros((levels, tiles, 8, LANES), F32)
+        ext[:, :, row0 : row0 + 8, :] = zero
+        for move in range(4):
+            shifted[move, :, :, row0 : row0 + 8, :] = zero
+        for k in range(2):
+            side[k, row0 : row0 + 8, :] = zero[0, 0]
+    stage[...] = jnp.zeros_like(stage)
+    cross[...] = jnp.zeros_like(cross)
+    padded = send_leg.shape[1]
+    basis[:, padded:, :] = jnp.zeros((half, HALF - padded, steps), BF16)
+    send_leg[:, rows:, :] = jnp.zeros((half, padded - rows, steps), BF16)
+
+    lane = at((rows, LANES), 1)
+    pltpu.make_async_copy(adv, adv, load_sem.at[0]).wait()
     for v in range(levels):
         for t in range(tiles):
-            cols = slice(t * LANES, (t + 1) * LANES)
-            pack_row[0, 2 * v : 2 * v + 2, cols] = ext[v, t + 1, 6 + rows : 8 + rows, :]
-            pack_row[1, 2 * v : 2 * v + 2, cols] = ext[v, t + 1, 8:10, :]
+            pack_row[0, t, 2 * v : 2 * v + 2, :] = ext[v, t, 6 + rows : 8 + rows, :]
+            pack_row[1, t, 2 * v : 2 * v + 2, :] = ext[v, t, 8:10, :]
     last = jnp.zeros((rows, LANES), F32)
     first = jnp.zeros((rows, LANES), F32)
     for v in range(levels):
-        here = (lane == 2 * v) | (lane == 2 * v + 1)
-        tail = pltpu.roll(ext[v, tiles, 8 : 8 + rows, :], (2 * v + 2) % LANES, 1)
-        last = jnp.where(here, tail, last)
-        head = ext[v, 1, 8 : 8 + rows, :]
-        if v:
-            head = pltpu.roll(head, 2 * v, 1)
-        first = jnp.where(here, head, first)
+        tail = pltpu.roll(ext[v, tiles - 1, 8 : 8 + rows, :], (2 * v + 2) % LANES, 1)
+        last = jnp.where(lax.div(lane, 2) == v, tail, last)
+        head = pltpu.roll(ext[v, 0, 8 : 8 + rows, :], HALF + 2 * v, 1)
+        first = jnp.where(lax.div(lane - HALF, 2) == v, head, first)
     pack_col[0] = last
     pack_col[1] = first
-
-    def shift_block(v, t, row0, size, moves=(-2, -1, 1, 2)):
-        at = pl.ds(row0, size)
-        at_lane = lax.broadcasted_iota(jnp.int32, (size, LANES), 1)
-        here = ext[v, t + 1, at, :]
-        left = ext[v, t, at, :] if min(moves) < 0 else None
-        right = ext[v, t + 2, at, :] if max(moves) > 0 else None
-        for move in moves:
-            n_move = (-2, -1, 1, 2).index(move)
-            amount = (-move) % LANES
-            mine = pltpu.roll(here, amount, 1)
-            if move < 0:
-                moved = jnp.where(at_lane < -move, pltpu.roll(left, amount, 1), mine)
-            else:
-                moved = jnp.where(at_lane >= LANES - move, pltpu.roll(right, amount, 1), mine)
-            shifted[n_move, v, t, at, :] = moved
-
-    def shift_inner(chosen):
-        def step(t, carry):
-            for v in chosen:
-                shift_block(v, t, 8, rows)
-            return carry
-
-        lax.fori_loop(1, tiles - 1, step, 0)
-
-    groups = rows // 8
-
-    def advect(t, chosen):
-        cols = pl.ds(pl.multiple_of(t * LANES, LANES), LANES)
-        corner = [wts[ab, :, cols].astype(F32) for ab in range(4)]
-        for g in chosen:
-            band = slice(8 * g, 8 * g + 8)
-            dr, dc = drow[band, cols], dcol[band, cols]
-            zero = jnp.zeros((8, LANES), F32)
-            in_col = {c: dc == c for c in range(-2, 2)}
-            in_row = {r: dr == r for r in range(-2, 2)}
-
-            def pick(masks, at, one, two):
-                value = zero
-                if at - 1 in masks:
-                    value = jnp.where(masks[at - 1], two, value)
-                if at in masks:
-                    value = jnp.where(masks[at], one, value)
-                return value
-
-            part = [
-                [pick(in_col, c, corner[2 * a][band], corner[2 * a + 1][band]) for c in range(-2, 3)]
-                for a in range(2)
-            ]
-            coef = [
-                [pick(in_row, r, part[0][c], part[1][c]) for c in range(5)] for r in range(-2, 3)
-            ]
-            for v in range(levels):
-                total = None
-                for r in range(5):
-                    at = pl.ds(8 * g + 6 + r, 8)
-                    for c in range(5):
-                        if c == 2:
-                            value = ext[v, t + 1, at, :]
-                        else:
-                            value = shifted[c if c < 2 else c - 1, v, t, at, :]
-                        term = coef[r][c] * value
-                        total = term if total is None else total + term
-                adv[v * rows + 8 * g : v * rows + 8 * g + 8, cols] = total
-
-    def advect_inner(t, carry):
-        advect(t, range(1, groups - 1))
-        return carry
-
-    pl.semaphore_wait(barrier, n - 1)
 
     def remote(src, dst, ssem, rsem, lat, lev):
         return pltpu.make_async_remote_copy(
@@ -201,65 +137,48 @@
             device_id=(lat, lev), device_id_type=MESH,
         )
 
-    def halo(n, src, dst, lat, lev):
-        return remote(src, dst, halo_send.at[n], halo_recv.at[n], lat, lev)
-
-    bottom, top = pl.ds(rows - 8, 8), pl.ds(0, 8)
+    def halo(k, src, dst, lat, lev):
+        return remote(src, dst, halo_send.at[k], halo_recv.at[k], lat, lev)
+
     flat = [
-        halo(0, pack_col.at[0], got_col.at[0], l, east),
-        halo(1, pack_col.at[1], got_col.at[1], l, west),
+        halo(2, pack_col.at[0], got_col.at[0], l, east),
+        halo(2, pack_col.at[1], got_col.at[1], l, west),
     ]
-    below = [
-        halo(2, pack_row.at[0], got_row.at[0], l + 1, e),
-        halo(3, pack_col.at[0, bottom], got_corner.at[0], l + 1, east),
-        halo(4, pack_col.at[1, bottom], got_corner.at[1], l + 1, west),
+    rims = [
+        [
+            halo(k, pack_row.at[k], got_rim.at[k, pl.ds(1, tiles)], lat, e),
+            halo(k, pack_row.at[k, tiles - 1], got_rim.at[k, 0], lat, east),
+            halo(k, pack_row.at[k, 0], got_rim.at[k, tiles + 1], lat, west),
+        ]
+        for k, lat in ((0, l + 1), (1, l - 1))
     ]
-    above = [
-        halo(5, pack_row.at[1], got_row.at[1], l - 1, e),
-        halo(6, pack_col.at[0, top], got_corner.at[2], l - 1, east),
-        halo(7, pack_col.at[1, top], got_corner.at[3], l - 1, west),
-    ]
+
+    pl.semaphore_wait(barrier, n - 1)
 
     @pl.when(has_down)
     def _():
-        for copy in below:
+        for copy in rims[0]:
             copy.start()
 
     @pl.when(has_up)
     def _():
-        for copy in above:
+        for copy in rims[1]:
             copy.start()
 
     for copy in flat:
         copy.start()
 
-    loads[tiles + 5].wait()
+    load_slot.wait()
     first = lax.broadcasted_iota(jnp.int32, (1, 4 * waves), 1)
     slot_row = jnp.zeros((1, 4 * waves), jnp.int32)
     for k in range(waves):
         slot_row = jnp.where(lax.rem(first, waves) == k, slot_ref[k], slot_row)
-    at = lambda shape, dim: lax.broadcasted_iota(jnp.int32, shape, dim)
     iota_f = (4 * waves, 4 * waves)
     order = one_hot(
         (lax.div(at(iota_f, 0), waves) == lax.div(at(iota_f, 1), waves))
         & (lax.rem(at(iota_f, 0), waves) == slot_row)
     )
-    stage[...] = jnp.zeros_like(stage)
-    cross[...] = jnp.zeros_like(cross)
-    padded = send_leg.shape[1]
-    basis[:, padded:, :] = jnp.zeros((half, HALF - padded, steps), BF16)
-
-    shift_inner(range(levels))
-    if tiles > 1:
-        for v in range(levels):
-            shift_block(v, 0, 8, rows, (1, 2))
-            shift_block(v, tiles - 1, 8, rows, (-2, -1))
-    for t in range(tiles, tiles + 3):
-        loads[t].wait()
-    lax.fori_loop(1, tiles - 1, advect_inner, 0)
-
-    loads[tiles + 4].wait()
-    send_leg[...] = jnp.zeros_like(send_leg)
+    load_leg.wait()
     band = 8
     iota_g = (half * band, band * waves)
     slot_cols = jnp.zeros((1, band * waves), jnp.int32)
@@ -288,76 +207,171 @@
         copies_g.append(copy)
     basis[lh, 0:padded, :] = send_leg[lh]
 
-    loads[tiles + 3].wait()
+    lane = at((8, LANES), 1)
+    moves = (-2, -1, 1, 2)
+
+    def move_blocks(blocks, move):
+        turned = [x if x is None else pltpu.roll(x, (-move) % LANES, 1) for x in blocks]
+        zero = jnp.zeros((8, LANES), F32)
+        result = []
+        for t in range(1, len(blocks) - 1):
+            near = turned[t - 1] if move < 0 else turned[t + 1]
+            wrapped = (lane < -move) if move < 0 else (lane >= LANES - move)
+            result.append(jnp.where(wrapped, zero if near is None else near, turned[t]))
+        return result
+
+    groups = rows // 8
+
+    def shift_level(v, carry):
+        for g in range(groups):
+            band = slice(8 + 8 * g, 16 + 8 * g)
+            blocks = [None] + [ext[v, t, band, :] for t in range(tiles)] + [None]
+            for k, move in enumerate(moves):
+                for t, value in enumerate(move_blocks(blocks, move)):
+                    shifted[k, v, t, band, :] = value
+        return carry
+
+    lax.fori_loop(0, levels, shift_level, 0)
+
+    def choose_two(high, low, values):
+        one = jnp.where(high, values[2], values[0])
+        two = jnp.where(high, values[3], values[1])
+        three = jnp.where(high, values[4], values[2])
+        return jnp.where(low, two, one), jnp.where(low, three, two)
+
+    load_wts.wait()
+    load_row.wait()
+    load_col.wait()
+
+    def advect(t, carry):
+        cols = pl.ds(pl.multiple_of(t * LANES, LANES), LANES)
+        corner = [points[k * rows : (k + 1) * rows, cols].astype(F32) for k in range(4)]
+        for g in range(groups):
+            band = slice(8 * g, 8 * g + 8)
+            dr, dc = drow[band, cols], dcol[band, cols]
+            row_high, row_low = dr >= 0, (dr & 1) == 1
+            col_high, col_low = dc >= 0, (dc & 1) == 1
+            w = [corner[k][band] for k in range(4)]
+            for v in range(levels):
+                picked = []
+                for c in range(5):
+                    ref = ext.at[v, t] if c == 2 else shifted.at[c if c < 2 else c - 1, v, t]
+                    picked.append(
+                        choose_two(
+                            row_high, row_low,
+                            [ref[8 * g + 6 + r : 8 * g + 14 + r, :] for r in range(5)],
+                        )
+                    )
+                upper = choose_two(col_high, col_low, [x[0] for x in picked])
+                lower = choose_two(col_high, col_low, [x[1] for x in picked])
+                total = w[0] * upper[0] + w[1] * upper[1] + w[2] * lower[0] + w[3] * lower[1]
+                adv[v * rows + 8 * g : v * rows + 8 * g + 8, cols] = total
+        return carry
+
+    lax.fori_loop(0, tiles, advect, 0)
+
+    load_tab.wait()
     tabs[...] = jnp.dot(order, tab[...], preferred_element_type=F32).astype(BF16)
 
-
-    def spread(piece, v):
-        return pltpu.roll(piece, LANES - 2 - 2 * v, 1)
-
-    def spread_east(piece, v):
-        return pltpu.roll(piece, LANES - 2 * v, 1) if v else piece
-
-    def rim(row0, size, from_west, from_east):
-        for v in range(levels):
-            ext[v, 0, row0 : row0 + size, :] = spread(from_west, v)
-            ext[v, tiles + 1, row0 : row0 + size, :] = spread_east(from_east, v)
-
-    def fill_rows(which, row0):
-        for v in range(levels):
+    points[4 * rows : 5 * rows, :] = drow[...].astype(F32).astype(BF16)
+    points[5 * rows : 6 * rows, :] = dcol[...].astype(F32).astype(BF16)
+    iota_r = (6 * 16, 6 * rows)
+    row_r, col_r = at(iota_r, 0), at(iota_r, 1)
+    odd = row_r & 1
+    repeat_rows = one_hot(
+        (lax.div(row_r, 16) == lax.div(col_r, rows))
+        & (lax.rem(col_r, rows) == jnp.where((row_r & 15) < 8, odd, rows - 2 + odd))
+    )
+    rim_points[...] = jnp.dot(repeat_rows, points[...], preferred_element_type=F32)
+    row_c, col_c = at((LANES, LANES), 0), at((LANES, LANES), 1)
+    from_first = one_hot((col_c < HALF) & (row_c == (col_c & 1)))
+    from_last = one_hot((col_c >= HALF) & (row_c == LANES - 2 + (col_c & 1)))
+    side_points[...] = jnp.dot(
+        points[:, 0:LANES], from_first, preferred_element_type=F32
+    ) + jnp.dot(points[:, width - LANES :], from_last, preferred_element_type=F32)
+
+    even = (at((8, LANES), 0) & 1) == 0
+
+    def fix_rows(k):
+        for c0 in range(0, 2 * levels, 8):
+            blocks = [got_rim[k, t, c0 : c0 + 8, :] for t in range(tiles + 2)]
+            moved = [move_blocks(blocks, move) for move in moves]
+            moved.insert(2, blocks[1:-1])
             for t in range(tiles):
                 cols = slice(t * LANES, (t + 1) * LANES)
-                ext[v, t + 1, row0 : row0 + 2, :] = got_row[which, 2 * v : 2 * v + 2, cols]
+                w0, w1, w2, w3, dr, dc = [
+                    rim_points[16 * q + 8 * k : 16 * q + 8 * k + 8, cols] for q in range(6)
+                ]
+                col_high, col_low = dc >= 0.0, (dc == -1.0) | (dc == 1.0)
+                same = [moved[c][t] for c in range(5)]
+                other = [pltpu.roll(x, 1 if k else 7, 0) for x in same]
+                s0, s1 = choose_two(col_high, col_low, same)
+                o0, o1 = choose_two(col_high, col_low, other)
+                if k == 0:
+                    far = jnp.where(dr == -2.0, w0 * s0 + w1 * s1, 0.0)
+                    near = jnp.where(
+                        dr == -1.0, w0 * o0 + w1 * o1,
+                        jnp.where(dr == -2.0, w2 * o0 + w3 * o1, 0.0),
+                    )
+                    near = jnp.where(even, near, 0.0)
+                else:
+                    far = jnp.where(dr == 1.0, w2 * s0 + w3 * s1, 0.0)
+                    near = jnp.where(
+                        dr == 1.0, w0 * o0 + w1 * o1,
+                        jnp.where(dr == 0.0, w2 * o0 + w3 * o1, 0.0),
+                    )
+                    near = jnp.where(even, 0.0, near)
+                extra = far + near
+                for i in range(0, 8, 2):
+                    row0 = (c0 + i) // 2 * rows + k * (rows - 2)
+                    adv[row0 : row0 + 2, cols] += extra[i : i + 2]
 
     @pl.when(has_up)
     def _():
-        for copy in below:
-            copy.wait_recv()
-        fill_rows(0, 6)
-        rim(0, 8, got_corner[0], got_corner[1])
-
-    @pl.when(jnp.logical_not(has_up))
-    def _():
-        ext[:, :, 0:8, :] = jnp.zeros((levels, tiles + 2, 8, LANES), F32)
+        pltpu.make_async_copy(got_rim.at[0], got_rim.at[0], halo_recv.at[0]).wait()
+        fix_rows(0)
 
     @pl.when(has_down)
     def _():
-        for copy in above:
-            copy.wait_recv()
-        fill_rows(1, rows + 8)
-        rim(rows + 8, 8, got_corner[2], got_corner[3])
-
-    @pl.when(jnp.logical_not(has_down))
-    def _():
-        ext[:, :, rows + 8 : rows + 16, :] = jnp.zeros((levels, tiles + 2, 8, LANES), F32)
-
-    for copy in flat:
-        copy.wait_recv()
-    rim(8, rows, got_col[0], got_col[1])
-
-    def shift_rims(t, carry):
+        pltpu.make_async_copy(got_rim.at[1], got_rim.at[1], halo_recv.at[1]).wait()
+        fix_rows(1)
+
+    pltpu.make_async_copy(got_col, got_col, halo_recv.at[2]).wait()
+    here = jnp.where(at((rows, LANES), 1) < HALF, got_col[0], got_col[1])
+    side[0, 8 : 8 + rows, :] = here
+    side[1, 8 : 8 + rows, :] = jnp.where(
+        at((rows, LANES), 1) < HALF, pltpu.roll(here, LANES - 1, 1), pltpu.roll(here, 1, 1)
+    )
+    in_west = lane < HALF
+    edge = jnp.where(in_west, -1.0, 1.0)
+    inner = (lane & 1) == jnp.where(in_west, 0, 1)
+    for g in range(groups):
+        w0, w1, w2, w3, dr, dc = [
+            side_points[q * rows + 8 * g : q * rows + 8 * g + 8, :] for q in range(6)
+        ]
+        row_high, row_low = dr >= 0.0, (dr == -1.0) | (dr == 1.0)
+        s0, s1 = choose_two(
+            row_high, row_low, [side[0, 8 * g + 6 + r : 8 * g + 14 + r, :] for r in range(5)]
+        )
+        o0, o1 = choose_two(
+            row_high, row_low, [side[1, 8 * g + 6 + r : 8 * g + 14 + r, :] for r in range(5)]
+        )
+        far = jnp.where(
+            dc == jnp.where(in_west, -2.0, 1.0),
+            jnp.where(in_west, w0, w1) * s0 + jnp.where(in_west, w2, w3) * s1,
+            0.0,
+        )
+        near = jnp.where(
+            dc == edge, w0 * o0 + w2 * o1,
+            jnp.where(dc == edge - 1.0, w1 * o0 + w3 * o1, 0.0),
+        )
+        extra = far + jnp.where(inner, near, 0.0)
         for v in range(levels):
-            shift_block(v, t, 0, 8)
-            shift_block(v, t, rows + 8, 8)
-        return carry
-
-    edges = min(tiles, 2)
-    for v in range(levels):
-        shift_block(v, 0, 8, rows, (-2, -1))
-        shift_block(v, tiles - 1, 8, rows, (1, 2))
-    lax.fori_loop(0, tiles, shift_rims, 0)
-    outer = sorted({0, groups - 1})
-
-    def advect_rims(t, carry):
-        advect(t, outer)
-        return carry
-
-    def advect_edge(n, carry):
-        advect(n * (tiles - 1), range(groups))
-        return carry
-
-    lax.fori_loop(0, edges, advect_edge, 0)
-    lax.fori_loop(1, tiles - 1, advect_rims, 0)
+            band = slice(v * rows + 8 * g, v * rows + 8 * g + 8)
+            west_part = pltpu.roll(extra, (LANES - 2 * v) % LANES, 1) if v else extra
+            adv[band, 0:LANES] += jnp.where(lane < 2, west_part, 0.0)
+            east_part = pltpu.roll(extra, (LANES - 2 - HALF - 2 * v) % LANES, 1)
+            adv[band, width - LANES :] += jnp.where(lane >= LANES - 2, east_part, 0.0)
 
     contract_last = (((1,), (1,)), ((), ()))
     for v in range(levels):
@@ -531,23 +545,17 @@
     for k in range(2 * own):
         spec_ref[k] = got_p[k]
 
-    for copy in flat:
-        copy.wait_send()
+    pltpu.make_async_copy(got_col, got_col, halo_send.at[2]).wait()
     pltpu.make_async_copy(legs, legs, leg_send).wait()
     all_of(got_1, one_send).wait()
     all_of(got_2, two_send).wait()
     pl.when(keeps)(all_of(send_p, p_send, lv - 1).wait)
     pl.when(jnp.logical_not(keeps))(all_of(send_p, p_send, lv).wait)
 
-    @pl.when(has_down)
-    def _():
-        for copy in below:
-            copy.wait_send()
-
-    @pl.when(has_up)
-    def _():
-        for copy in above:
-            copy.wait_send()
+    for k, there in ((0, has_down), (1, has_up)):
+        pl.when(there)(
+            pltpu.make_async_copy(got_rim.at[k], got_rim.at[k], halo_send.at[k]).wait
+        )
 
 
 def finish(adv, synth, wide, spec, out_hbm, spec_hbm, lead_all, rest_all, result, sems):
@@ -612,19 +620,21 @@
             out_specs=(in_vmem,) * 4,
             scratch_shapes=[
                 pltpu.SMEM((waves,), jnp.int32),
-                vmem((levels, tiles + 2, rows + 16, LANES), F32),
+                vmem((levels, tiles, rows + 16, LANES), F32),
                 vmem((4, levels, tiles, rows + 16, LANES), F32),
-                vmem((4, rows, width), BF16),
+                vmem((6 * rows, width), BF16),
                 vmem((rows, width), jnp.int32),
                 vmem((rows, width), jnp.int32),
                 vmem((rows * waves, steps), BF16),
                 vmem((4 * waves, width), BF16),
                 vmem((4 * waves, width), BF16),
-                vmem((2, 2 * levels, width), F32),
+                vmem((2, tiles, 2 * levels, LANES), F32),
                 vmem((2, rows, LANES), F32),
-                vmem((2, 2 * levels, width), F32),
+                vmem((2, tiles + 2, 2 * levels, LANES), F32),
                 vmem((2, rows, LANES), F32),
-                vmem((4, 8, LANES), F32),
+                vmem((6 * 16, width), F32),
+                vmem((6 * rows, LANES), F32),
+                vmem((2, rows + 16, LANES), F32),
                 vmem((half, -(-rows // 16) * 16, steps), BF16),
                 vmem((half, HALF, steps), BF16),
                 vmem((2 * pairs, LANES), F32),
@@ -637,8 +647,8 @@
                 vmem((2, 2 * pairs, 4 * LANES), BF16),
                 vmem((lv, 2, steps), F32),
                 vmem((2 * own, 2, steps), F32),
-                dma((tiles + 6,)),
-                dma((8,)), dma((8,)),
+                dma((7,)),
+                dma((3,)), dma((3,)),
                 dma, dma,
                 dma, dma,
                 dma, dma,
@@ -651,7 +661,7 @@
             *(
                 pltpu.with_memory_space_constraint(x, pltpu.HBM)
                 for x in (
-                    wave_slot, field, weights, depart_row, depart_col,
+                    wave_slot, field, weights.reshape(4 * rows, width), depart_row, depart_col,
                     legendre.reshape(rows * waves, steps), table,
                 )
             ),

time: 25.8 us -> 24.7 us (0.957)
  Pallas kernels: 25 us -> 23.9 us
    pallas_call x1, Pallas kernels: 23.9 us -> 22.7 us  [on_device(): pl.pallas_call(functools.partial(kernel, n_lat, n_lev), out_shape=(vmem((...]
where the time goes in v3:
time: 24.7 us; the launch traced here: 24.5 us
  Pallas kernels  23.9 us (97%)
  between operations  0.64 us (3%)
    pallas_call x1, Pallas kernels, on_device(): pl.pallas_call(functools.partial(kernel, n_lat, n_lev), out_shape=(vmem((...  22.7 us
    pallas_call x1, Pallas kernels, on_device(): pl.pallas_call(finish, out_shape=(jax.ShapeDtypeStruct((levels, rows, wid...  1.18 us

profile of v3, /device:TPU:0, one launch (start us, length us, event | category | flops | bytes accessed | tf_op | source)
XLA Modules:
  0.0 24.5 jit_solution(14689097980016142668)
XLA Ops:
  0.6 22.7 %shard_map.86 = (f32[160,1024]{1,0:T(8,128)S(1)}, f32[40,128]{1,0:T(8,128)S(1)}, bf16[2,128,1024]{2,1,0:T(8,128)(2,1)S(1)}, f32[4,2,640]{2,1,0:T(2,128)S(1)}) custom-call(s32[16]{0:T(128)} %slot_hbm.1, f32[4,40,1024]{2,1,0:T(8,128)} %field_hbm.1, bf16[160,1024]{1,0:T(8,128)(2,1)} %bitcast.6, s32[40,1024]{1,0:T(8,128)} %drow_hbm.1, s32[40,1024]{1,0:T(8,128)} %dcol_hbm.1, ...), custom_call_target="tpu_custom_call" | custom-call | tf_op jit(solution)/shard_map/pallas_call | solution.py:611
  23.4 1.2 %shard_map.87 = (f32[4,40,1024]{2,1,0:T(8,128)}, f32[4,2,640]{2,1,0:T(2,128)}) custom-call(f32[160,1024]{1,0:T(8,128)S(1)} %get-tuple-element.8.adv, f32[40,128]{1,0:T(8,128)S(1)} %get-tuple-element.9.synth, bf16[2,128,1024]{2,1,0:T(8,128)(2,1)S(1)} %get-tuple-element.10.wide, f32[4,2,640]{2,1,0:T(2,128)S(1)} %get-tuple-element.11.spec), custom_call_target="tpu_custom_call" | custom-call | tf_op jit(solution)/shard_map/pallas_call | solution.py:670

commit v4 on v3

--- a/solution.py
+++ b/solution.py
@@ -53,7 +53,7 @@
     pack_row, pack_col, got_rim, got_col, rim_points, side_points, side,
     send_leg, basis, stage, send_1, got_1, both_f, both_b, send_2, got_2, cross, send_p, got_p,
     load_sem, halo_send, halo_recv, leg_send, leg_recv, one_send, one_recv,
-    two_send, two_recv, p_send, p_recv,
+    two_send, two_recv, p_send, p_recv, round_sem,
 ):
     levels, _, _, _ = ext.shape
     rows, width = drow.shape
@@ -96,10 +96,42 @@
 
     barrier = pltpu.get_barrier_semaphore()
 
-    @each(1, n)
-    def _(off):
-        lat, lev = device(off)
+    def greet(lat, lev):
         pl.semaphore_signal(barrier, inc=1, device_id=(lat, lev), device_id_type=MESH)
+
+    def flipped(i, bit):
+        return i + bit - 2 * bit * lax.rem(lax.div(i, bit), 2)
+
+    bits = lambda size: [1 << k for k in range((size - 1).bit_length())]
+    rounds = [(l, flipped(e, bit)) for bit in bits(n_lev)]
+    rounds += [(flipped(l, bit), e) for bit in bits(n_lat)]
+    partners = [(l, east), (l, west), (flipped(l, half), e)]
+    partners += [(l, flipped(e, bit)) for bit in bits(n_lev)[1:]]
+    partners += [(parity * half + lax.rem(lh + off, half), e) for off in range(1, half)]
+    for there, lat in ((has_down, l + 1), (has_up, l - 1)):
+
+        @pl.when(there)
+        def _():
+            for lev in (e, east, west):
+                greet(lat, lev)
+
+    for lat, lev in partners:
+        greet(lat, lev)
+    n_greet = len(partners) + jnp.where(has_up, 3, 0) + jnp.where(has_down, 3, 0)
+
+    passed = []
+
+    def advance():
+        k = len(passed)
+        if k > len(rounds):
+            return
+        if k:
+            pl.semaphore_wait(round_sem.at[k - 1], 1)
+        if k < len(rounds):
+            pl.semaphore_signal(
+                round_sem.at[k], inc=1, device_id=rounds[k], device_id_type=MESH
+            )
+        passed.append(k)
 
     at = lambda shape, dim: lax.broadcasted_iota(jnp.int32, shape, dim)
     for row0 in (0, rows + 8):
@@ -153,7 +185,7 @@
         for k, lat in ((0, l + 1), (1, l - 1))
     ]
 
-    pl.semaphore_wait(barrier, n - 1)
+    pl.semaphore_wait(barrier, n_greet)
 
     @pl.when(has_down)
     def _():
@@ -168,6 +200,7 @@
     for copy in flat:
         copy.start()
 
+    advance()
     load_slot.wait()
     first = lax.broadcasted_iota(jnp.int32, (1, 4 * waves), 1)
     slot_row = jnp.zeros((1, 4 * waves), jnp.int32)
@@ -207,6 +240,7 @@
         copies_g.append(copy)
     basis[lh, 0:padded, :] = send_leg[lh]
 
+    advance()
     lane = at((8, LANES), 1)
     moves = (-2, -1, 1, 2)
 
@@ -239,36 +273,59 @@
         three = jnp.where(high, values[4], values[2])
         return jnp.where(low, two, one), jnp.where(low, three, two)
 
+    advance()
     load_wts.wait()
     load_row.wait()
     load_col.wait()
 
+    sub = at((8, LANES), 0)
+
     def advect(t, carry):
         cols = pl.ds(pl.multiple_of(t * LANES, LANES), LANES)
         corner = [points[k * rows : (k + 1) * rows, cols].astype(F32) for k in range(4)]
-        for g in range(groups):
-            band = slice(8 * g, 8 * g + 8)
-            dr, dc = drow[band, cols], dcol[band, cols]
-            row_high, row_low = dr >= 0, (dr & 1) == 1
-            col_high, col_low = dc >= 0, (dc & 1) == 1
-            w = [corner[k][band] for k in range(4)]
-            for v in range(levels):
-                picked = []
-                for c in range(5):
-                    ref = ext.at[v, t] if c == 2 else shifted.at[c if c < 2 else c - 1, v, t]
-                    picked.append(
-                        choose_two(
-                            row_high, row_low,
-                            [ref[8 * g + 6 + r : 8 * g + 14 + r, :] for r in range(5)],
-                        )
-                    )
+        zero = jnp.zeros((8, LANES), F32)
+        turned = {}
+
+        def turn(v, c, g, amount):
+            if g < 0 or g >= groups:
+                return zero
+            key = (v, c, g, amount)
+            if key not in turned:
+                turned[key] = pltpu.roll(plane(v, c)[8 * g + 8 : 8 * g + 16, :], amount, 0)
+            return turned[key]
+
+        def plane(v, c):
+            return ext.at[v, t] if c == 2 else shifted.at[c if c < 2 else c - 1, v, t]
+
+        def five(v, c, g):
+            ref = plane(v, c)
+            load_at = lambda r: ref[8 * g + 8 + r : 8 * g + 16 + r, :]
+            values = [load_at(r) for r in (-1, 0, 1)]
+            if c in (0, 1, 3, 4):
+                before = jnp.where(sub < 2, turn(v, c, g - 1, 2), turn(v, c, g, 2))
+                after = jnp.where(sub < 6, turn(v, c, g, 6), turn(v, c, g + 1, 6))
+            else:
+                before, after = load_at(-2), load_at(2)
+            return [before] + values + [after]
+
+        for v in range(levels):
+            for g in range(groups):
+                band = slice(8 * g, 8 * g + 8)
+                dr, dc = drow[band, cols], dcol[band, cols]
+                row_high, row_low = dr >= 0, (dr & 1) == 1
+                col_high, col_low = dc >= 0, (dc & 1) == 1
+                w = [corner[k][band] for k in range(4)]
+                picked = [choose_two(row_high, row_low, five(v, c, g)) for c in range(5)]
                 upper = choose_two(col_high, col_low, [x[0] for x in picked])
                 lower = choose_two(col_high, col_low, [x[1] for x in picked])
                 total = w[0] * upper[0] + w[1] * upper[1] + w[2] * lower[0] + w[3] * lower[1]
                 adv[v * rows + 8 * g : v * rows + 8 * g + 8, cols] = total
         return carry
 
-    lax.fori_loop(0, tiles, advect, 0)
+    lax.fori_loop(0, tiles // 2, advect, 0)
+    advance()
+    lax.fori_loop(tiles // 2, tiles, advect, 0)
+    advance()
 
     load_tab.wait()
     tabs[...] = jnp.dot(order, tab[...], preferred_element_type=F32).astype(BF16)
@@ -396,6 +453,9 @@
         return remote(
             send_1.at[owner], got_1.at[me], one_send, one_recv, lat, lev
         )
+
+    while len(passed) <= len(rounds):
+        advance()
 
     @each(1, n)
     def _(off):
@@ -653,6 +713,9 @@
                 dma, dma,
                 dma, dma,
                 dma, dma,
+                pltpu.SemaphoreType.REGULAR(
+                    ((n_lev - 1).bit_length() + (n_lat - 1).bit_length(),)
+                ),
             ],
             compiler_params=pltpu.CompilerParams(
                 collective_id=0, has_side_effects=True, vmem_limit_bytes=40 << 20

time: 24.7 us -> 23 us (0.931)
  Pallas kernels: 23.9 us -> 22.2 us
    pallas_call x1, Pallas kernels: 22.7 us -> 21 us  [on_device(): pl.pallas_call(functools.partial(kernel, n_lat, n_lev), out_shape=(vmem((...]
where the time goes in v4:
time: 23 us; the launch traced here: 22.8 us
  Pallas kernels  22.2 us (97%)
  between operations  0.64 us (3%)
    pallas_call x1, Pallas kernels, on_device(): pl.pallas_call(functools.partial(kernel, n_lat, n_lev), out_shape=(vmem((...  21 us
    pallas_call x1, Pallas kernels, on_device(): pl.pallas_call(finish, out_shape=(jax.ShapeDtypeStruct((levels, rows, wid...  1.17 us

profile of v4, /device:TPU:0, one launch (start us, length us, event | category | flops | bytes accessed | tf_op | source)
XLA Modules:
  0.0 22.8 jit_solution(14346000833086539059)
XLA Ops:
  0.6 21.0 %shard_map.86 = (f32[160,1024]{1,0:T(8,128)S(1)}, f32[40,128]{1,0:T(8,128)S(1)}, bf16[2,128,1024]{2,1,0:T(8,128)(2,1)S(1)}, f32[4,2,640]{2,1,0:T(2,128)S(1)}) custom-call(s32[16]{0:T(128)} %slot_hbm.1, f32[4,40,1024]{2,1,0:T(8,128)} %field_hbm.1, bf16[160,1024]{1,0:T(8,128)(2,1)} %bitcast.6, s32[40,1024]{1,0:T(8,128)} %drow_hbm.1, s32[40,1024]{1,0:T(8,128)} %dcol_hbm.1, ...), custom_call_target="tpu_custom_call" | custom-call | tf_op jit(solution)/shard_map/pallas_call | solution.py:671
  21.6 1.2 %shard_map.87 = (f32[4,40,1024]{2,1,0:T(8,128)}, f32[4,2,640]{2,1,0:T(2,128)}) custom-call(f32[160,1024]{1,0:T(8,128)S(1)} %get-tuple-element.8.adv, f32[40,128]{1,0:T(8,128)S(1)} %get-tuple-element.9.synth, bf16[2,128,1024]{2,1,0:T(8,128)(2,1)S(1)} %get-tuple-element.10.wide, f32[4,2,640]{2,1,0:T(2,128)S(1)} %get-tuple-element.11.spec), custom_call_target="tpu_custom_call" | custom-call | tf_op jit(solution)/shard_map/pallas_call | solution.py:733

commit v5 on v4

--- a/solution.py
+++ b/solution.py
@@ -50,7 +50,7 @@
     slot_hbm, field_hbm, weights_hbm, drow_hbm, dcol_hbm, leg_hbm, table_hbm,
     adv, synth, wide, spec_ref,
     slot_ref, ext, shifted, points, drow, dcol, leg, tab, tabs,
-    pack_row, pack_col, got_rim, got_col, rim_points, side_points, side,
+    rim_rows, pack_row, pack_col, got_rim, got_col, rim_inputs, rim_points, side_points, side,
     send_leg, basis, stage, send_1, got_1, both_f, both_b, send_2, got_2, cross, send_p, got_p,
     load_sem, halo_send, halo_recv, leg_send, leg_recv, one_send, one_recv,
     two_send, two_recv, p_send, p_recv, round_sem,
@@ -74,10 +74,6 @@
     has_up, has_down = l > 0, l < n_lat - 1
     east, west = lax.rem(e + 1, n_lev), lax.rem(e + n_lev - 1, n_lev)
 
-    def device(off):
-        d = lax.rem(me + off, n)
-        return lax.div(d, n_lev), lax.rem(d, n_lev)
-
     def load(k, src, dst):
         copy = pltpu.make_async_copy(src, dst, load_sem.at[k])
         copy.start()
@@ -88,6 +84,12 @@
     load_leg = load(1, leg_hbm, leg)
     load_slot = load(2, slot_hbm, slot_ref)
     load_wts = load(3, weights_hbm, points.at[pl.ds(0, 4 * rows), :])
+    for q in range(4):
+        for k in range(2):
+            load(
+                7, weights_hbm.at[pl.ds(q * rows + k * (rows - 8), 8), :],
+                rim_inputs.at[pl.ds(16 * q + 8 * k, 8), :],
+            )
     load_row = load(4, drow_hbm, drow)
     load_col = load(5, dcol_hbm, dcol)
     load_tab = load(
@@ -99,15 +101,10 @@
     def greet(lat, lev):
         pl.semaphore_signal(barrier, inc=1, device_id=(lat, lev), device_id_type=MESH)
 
-    def flipped(i, bit):
-        return i + bit - 2 * bit * lax.rem(lax.div(i, bit), 2)
-
-    bits = lambda size: [1 << k for k in range((size - 1).bit_length())]
-    rounds = [(l, flipped(e, bit)) for bit in bits(n_lev)]
-    rounds += [(flipped(l, bit), e) for bit in bits(n_lat)]
-    partners = [(l, east), (l, west), (flipped(l, half), e)]
-    partners += [(l, flipped(e, bit)) for bit in bits(n_lev)[1:]]
-    partners += [(parity * half + lax.rem(lh + off, half), e) for off in range(1, half)]
+    column = [(parity * half + lax.rem(lh + off, half), e) for off in range(1, half)]
+    across = (lax.rem(l + half, n_lat), e)
+    partners = [(l, lax.rem(e + off, n_lev)) for off in range(1, n_lev)]
+    partners += column + [across]
     for there, lat in ((has_down, l + 1), (has_up, l - 1)):
 
         @pl.when(there)
@@ -119,19 +116,9 @@
         greet(lat, lev)
     n_greet = len(partners) + jnp.where(has_up, 3, 0) + jnp.where(has_down, 3, 0)
 
-    passed = []
-
-    def advance():
-        k = len(passed)
-        if k > len(rounds):
-            return
-        if k:
-            pl.semaphore_wait(round_sem.at[k - 1], 1)
-        if k < len(rounds):
-            pl.semaphore_signal(
-                round_sem.at[k], inc=1, device_id=rounds[k], device_id_type=MESH
-            )
-        passed.append(k)
+    def tell(k, devices):
+        for there in devices:
+            pl.semaphore_signal(round_sem.at[k], inc=1, device_id=there, device_id_type=MESH)
 
     at = lambda shape, dim: lax.broadcasted_iota(jnp.int32, shape, dim)
     for row0 in (0, rows + 8):
@@ -145,14 +132,14 @@
     cross[...] = jnp.zeros_like(cross)
     padded = send_leg.shape[1]
     basis[:, padded:, :] = jnp.zeros((half, HALF - padded, steps), BF16)
-    send_leg[:, rows:, :] = jnp.zeros((half, padded - rows, steps), BF16)
 
     lane = at((rows, LANES), 1)
     pltpu.make_async_copy(adv, adv, load_sem.at[0]).wait()
     for v in range(levels):
         for t in range(tiles):
-            pack_row[0, t, 2 * v : 2 * v + 2, :] = ext[v, t, 6 + rows : 8 + rows, :]
-            pack_row[1, t, 2 * v : 2 * v + 2, :] = ext[v, t, 8:10, :]
+            rim_rows[0, t, 2 * v : 2 * v + 2, :] = ext[v, t, 6 + rows : 8 + rows, :]
+            rim_rows[1, t, 2 * v : 2 * v + 2, :] = ext[v, t, 8:10, :]
+    pack_row[...] = rim_rows[...].astype(BF16)
     last = jnp.zeros((rows, LANES), F32)
     first = jnp.zeros((rows, LANES), F32)
     for v in range(levels):
@@ -160,8 +147,8 @@
         last = jnp.where(lax.div(lane, 2) == v, tail, last)
         head = pltpu.roll(ext[v, 0, 8 : 8 + rows, :], HALF + 2 * v, 1)
         first = jnp.where(lax.div(lane - HALF, 2) == v, head, first)
-    pack_col[0] = last
-    pack_col[1] = first
+    pack_col[0] = last.astype(BF16)
+    pack_col[1] = first.astype(BF16)
 
     def remote(src, dst, ssem, rsem, lat, lev):
         return pltpu.make_async_remote_copy(
@@ -200,7 +187,34 @@
     for copy in flat:
         copy.start()
 
-    advance()
+    tell(0, column)
+
+    lane = at((8, LANES), 1)
+    moves = (-2, -1, 1, 2)
+
+    def move_blocks(blocks, move):
+        turned = [x if x is None else pltpu.roll(x, (-move) % LANES, 1) for x in blocks]
+        zero = jnp.zeros((8, LANES), F32)
+        result = []
+        for t in range(1, len(blocks) - 1):
+            near = turned[t - 1] if move < 0 else turned[t + 1]
+            wrapped = (lane < -move) if move < 0 else (lane >= LANES - move)
+            result.append(jnp.where(wrapped, zero if near is None else near, turned[t]))
+        return result
+
+    groups = rows // 8
+
+    def shift_level(v):
+        for g in range(groups):
+            band = slice(8 + 8 * g, 16 + 8 * g)
+            blocks = [None] + [ext[v, t, band, :] for t in range(tiles)] + [None]
+            for k, move in enumerate(moves):
+                for t, value in enumerate(move_blocks(blocks, move)):
+                    shifted[k, v, t, band, :] = value
+
+    for v in range(levels):
+        shift_level(v)
+
     load_slot.wait()
     first = lax.broadcasted_iota(jnp.int32, (1, 4 * waves), 1)
     slot_row = jnp.zeros((1, 4 * waves), jnp.int32)
@@ -240,40 +254,12 @@
         copies_g.append(copy)
     basis[lh, 0:padded, :] = send_leg[lh]
 
-    advance()
-    lane = at((8, LANES), 1)
-    moves = (-2, -1, 1, 2)
-
-    def move_blocks(blocks, move):
-        turned = [x if x is None else pltpu.roll(x, (-move) % LANES, 1) for x in blocks]
-        zero = jnp.zeros((8, LANES), F32)
-        result = []
-        for t in range(1, len(blocks) - 1):
-            near = turned[t - 1] if move < 0 else turned[t + 1]
-            wrapped = (lane < -move) if move < 0 else (lane >= LANES - move)
-            result.append(jnp.where(wrapped, zero if near is None else near, turned[t]))
-        return result
-
-    groups = rows // 8
-
-    def shift_level(v, carry):
-        for g in range(groups):
-            band = slice(8 + 8 * g, 16 + 8 * g)
-            blocks = [None] + [ext[v, t, band, :] for t in range(tiles)] + [None]
-            for k, move in enumerate(moves):
-                for t, value in enumerate(move_blocks(blocks, move)):
-                    shifted[k, v, t, band, :] = value
-        return carry
-
-    lax.fori_loop(0, levels, shift_level, 0)
-
     def choose_two(high, low, values):
         one = jnp.where(high, values[2], values[0])
         two = jnp.where(high, values[3], values[1])
         three = jnp.where(high, values[4], values[2])
         return jnp.where(low, two, one), jnp.where(low, three, two)
 
-    advance()
     load_wts.wait()
     load_row.wait()
     load_col.wait()
@@ -323,23 +309,30 @@
         return carry
 
     lax.fori_loop(0, tiles // 2, advect, 0)
-    advance()
+    pl.semaphore_wait(round_sem.at[0], half - 1)
+    tell(1, [across])
     lax.fori_loop(tiles // 2, tiles, advect, 0)
-    advance()
 
     load_tab.wait()
     tabs[...] = jnp.dot(order, tab[...], preferred_element_type=F32).astype(BF16)
 
-    points[4 * rows : 5 * rows, :] = drow[...].astype(F32).astype(BF16)
-    points[5 * rows : 6 * rows, :] = dcol[...].astype(F32).astype(BF16)
-    iota_r = (6 * 16, 6 * rows)
+    weights_in = rim_inputs.at[pl.ds(0, 64), :]
+    pltpu.make_async_copy(weights_in, weights_in, load_sem.at[7]).wait()
+    for q, ref in ((4, drow), (5, dcol)):
+        for k in range(2):
+            row0 = 16 * q + 8 * k
+            rim_inputs[row0 : row0 + 8, :] = (
+                ref[k * (rows - 8) : k * (rows - 8) + 8, :].astype(F32).astype(BF16)
+            )
+        for cols in (slice(0, LANES), slice(width - LANES, width)):
+            points[q * rows : (q + 1) * rows, cols] = ref[:, cols].astype(F32).astype(BF16)
+    iota_r = (6 * 16, 6 * 16)
     row_r, col_r = at(iota_r, 0), at(iota_r, 1)
-    odd = row_r & 1
     repeat_rows = one_hot(
-        (lax.div(row_r, 16) == lax.div(col_r, rows))
-        & (lax.rem(col_r, rows) == jnp.where((row_r & 15) < 8, odd, rows - 2 + odd))
-    )
-    rim_points[...] = jnp.dot(repeat_rows, points[...], preferred_element_type=F32)
+        (lax.div(row_r, 8) == lax.div(col_r, 8))
+        & ((col_r & 7) == (row_r & 1) + jnp.where((row_r & 15) < 8, 0, 6))
+    )
+    rim_points[...] = jnp.dot(repeat_rows, rim_inputs[...], preferred_element_type=F32)
     row_c, col_c = at((LANES, LANES), 0), at((LANES, LANES), 1)
     from_first = one_hot((col_c < HALF) & (row_c == (col_c & 1)))
     from_last = one_hot((col_c >= HALF) & (row_c == LANES - 2 + (col_c & 1)))
@@ -351,7 +344,7 @@
 
     def fix_rows(k):
         for c0 in range(0, 2 * levels, 8):
-            blocks = [got_rim[k, t, c0 : c0 + 8, :] for t in range(tiles + 2)]
+            blocks = [got_rim[k, t, c0 : c0 + 8, :].astype(F32) for t in range(tiles + 2)]
             moved = [move_blocks(blocks, move) for move in moves]
             moved.insert(2, blocks[1:-1])
             for t in range(tiles):
@@ -394,7 +387,9 @@
         fix_rows(1)
 
     pltpu.make_async_copy(got_col, got_col, halo_recv.at[2]).wait()
-    here = jnp.where(at((rows, LANES), 1) < HALF, got_col[0], got_col[1])
+    here = jnp.where(
+        at((rows, LANES), 1) < HALF, got_col[0].astype(F32), got_col[1].astype(F32)
+    )
     side[0, 8 : 8 + rows, :] = here
     side[1, 8 : 8 + rows, :] = jnp.where(
         at((rows, LANES), 1) < HALF, pltpu.roll(here, LANES - 1, 1), pltpu.roll(here, 1, 1)
@@ -447,19 +442,30 @@
         for g in range(rep):
             send_1[s * rep + g] = stage[pl.ds(g * lv * waves + s, lv, stride=waves), :]
 
-    def copy_1(off):
-        lat, lev = device(off)
-        owner = lax.rem(lat, half) * n_lev + lev
-        return remote(
-            send_1.at[owner], got_1.at[me], one_send, one_recv, lat, lev
-        )
-
-    while len(passed) <= len(rounds):
-        advance()
-
-    @each(1, n)
-    def _(off):
-        copy_1(off).start()
+    turn_by = jnp.where(parity == 0, n_lat - 1, 1)
+
+    def others(body):
+        def column_of(a, first):
+            lat = lax.rem(l + turn_by * a, n_lat)
+            inside = lax.div(lat, half) == parity
+            block = jnp.where(inside, lat, n_lat - 1 - lat) - parity * half
+            base = lax.rem(lat, half) * n_lev
+
+            def send(b):
+                lev = lax.rem(e + b, n_lev)
+                body(lat, lev, base + lev, block)
+
+            each(first, n_lev)(send)
+
+        each(1, n_lat)(lambda a: column_of(a, 0))
+        column_of(0, 1)
+
+    def start_1(lat, lev, owner, block):
+        remote(send_1.at[owner], got_1.at[me], one_send, one_recv, lat, lev).start()
+
+    pl.semaphore_wait(round_sem.at[1], 1)
+
+    others(start_1)
 
     got_1[me] = send_1[lh * n_lev + e]
 
@@ -546,17 +552,10 @@
         send_2[b] = jnp.where(low, real, pltpu.roll(imag, HALF, 1))
         send_2[b + 1] = jnp.where(low, pltpu.roll(real, HALF, 1), imag)
 
-    def copy_2(off):
-        lat, lev = device(off)
-        inside = lax.div(lat, half) == parity
-        block = jnp.where(inside, lat, n_lat - 1 - lat) - parity * half
-        return remote(
-            send_2.at[block], got_2.at[me], two_send, two_recv, lat, lev
-        )
-
-    @each(1, n)
-    def _(off):
-        copy_2(off).start()
+    def start_2(lat, lev, owner, block):
+        remote(send_2.at[block], got_2.at[me], two_send, two_recv, lat, lev).start()
+
+    others(start_2)
 
     got_2[me] = send_2[lh]
 
@@ -689,13 +688,15 @@
                 vmem((4 * waves, width), BF16),
                 vmem((4 * waves, width), BF16),
                 vmem((2, tiles, 2 * levels, LANES), F32),
-                vmem((2, rows, LANES), F32),
-                vmem((2, tiles + 2, 2 * levels, LANES), F32),
-                vmem((2, rows, LANES), F32),
+                vmem((2, tiles, 2 * levels, LANES), BF16),
+                vmem((2, rows, LANES), BF16),
+                vmem((2, tiles + 2, 2 * levels, LANES), BF16),
+                vmem((2, rows, LANES), BF16),
+                vmem((6 * 16, width), BF16),
                 vmem((6 * 16, width), F32),
                 vmem((6 * rows, LANES), F32),
                 vmem((2, rows + 16, LANES), F32),
-                vmem((half, -(-rows // 16) * 16, steps), BF16),
+                vmem((half, rows, steps), BF16),
                 vmem((half, HALF, steps), BF16),
                 vmem((2 * pairs, LANES), F32),
                 vmem((owners, lv, LANES), F32),
@@ -707,15 +708,13 @@
                 vmem((2, 2 * pairs, 4 * LANES), BF16),
                 vmem((lv, 2, steps), F32),
                 vmem((2 * own, 2, steps), F32),
-                dma((7,)),
+                dma((8,)),
                 dma((3,)), dma((3,)),
                 dma, dma,
                 dma, dma,
                 dma, dma,
                 dma, dma,
-                pltpu.SemaphoreType.REGULAR(
-                    ((n_lev - 1).bit_length() + (n_lat - 1).bit_length(),)
-                ),
+                pltpu.SemaphoreType.REGULAR((2,)),
             ],
             compiler_params=pltpu.CompilerParams(
                 collective_id=0, has_side_effects=True, vmem_limit_bytes=40 << 20

time: 23 us -> 21.3 us (0.926)
  Pallas kernels: 22.2 us -> 20.5 us
    pallas_call x1, Pallas kernels: 21 us -> 19.3 us  [on_device(): pl.pallas_call(functools.partial(kernel, n_lat, n_lev), out_shape=(vmem((...]
where the time goes in v5:
time: 21.3 us; the launch traced here: 21.1 us
  Pallas kernels  20.5 us (96%)
  between operations  0.64 us (3%)
    pallas_call x1, Pallas kernels, on_device(): pl.pallas_call(functools.partial(kernel, n_lat, n_lev), out_shape=(vmem((...  19.3 us
    pallas_call x1, Pallas kernels, on_device(): pl.pallas_call(finish, out_shape=(jax.ShapeDtypeStruct((levels, rows, wid...  1.17 us

profile of v5, /device:TPU:0, one launch (start us, length us, event | category | flops | bytes accessed | tf_op | source)
XLA Modules:
  0.0 21.1 jit_solution(1794076387921943975)
XLA Ops:
  0.6 19.3 %shard_map.86 = (f32[160,1024]{1,0:T(8,128)S(1)}, f32[40,128]{1,0:T(8,128)S(1)}, bf16[2,128,1024]{2,1,0:T(8,128)(2,1)S(1)}, f32[4,2,640]{2,1,0:T(2,128)S(1)}) custom-call(s32[16]{0:T(128)} %slot_hbm.1, f32[4,40,1024]{2,1,0:T(8,128)} %field_hbm.1, bf16[160,1024]{1,0:T(8,128)(2,1)} %bitcast.6, s32[40,1024]{1,0:T(8,128)} %drow_hbm.1, s32[40,1024]{1,0:T(8,128)} %dcol_hbm.1, ...), custom_call_target="tpu_custom_call" | custom-call | tf_op jit(solution)/shard_map/pallas_call | solution.py:670
  20.0 1.2 %shard_map.87 = (f32[4,40,1024]{2,1,0:T(8,128)}, f32[4,2,640]{2,1,0:T(2,128)}) custom-call(f32[160,1024]{1,0:T(8,128)S(1)} %get-tuple-element.8.adv, f32[40,128]{1,0:T(8,128)S(1)} %get-tuple-element.9.synth, bf16[2,128,1024]{2,1,0:T(8,128)(2,1)S(1)} %get-tuple-element.10.wide, f32[4,2,640]{2,1,0:T(2,128)S(1)} %get-tuple-element.11.spec), custom_call_target="tpu_custom_call" | custom-call | tf_op jit(solution)/shard_map/pallas_call | solution.py:732

commit v6 on v5

--- a/solution.py
+++ b/solution.py
@@ -51,7 +51,7 @@
     adv, synth, wide, spec_ref,
     slot_ref, ext, shifted, points, drow, dcol, leg, tab, tabs,
     rim_rows, pack_row, pack_col, got_rim, got_col, rim_inputs, rim_points, side_points, side,
-    send_leg, basis, stage, send_1, got_1, both_f, both_b, send_2, got_2, cross, send_p, got_p,
+    send_leg, basis, stage, send_1, got_1, both_f, send_2, got_2, cross, send_p, got_p,
     load_sem, halo_send, halo_recv, leg_send, leg_recv, one_send, one_recv,
     two_send, two_recv, p_send, p_recv, round_sem,
 ):
@@ -74,13 +74,42 @@
     has_up, has_down = l > 0, l < n_lat - 1
     east, west = lax.rem(e + 1, n_lev), lax.rem(e + n_lev - 1, n_lev)
 
+    barrier = pltpu.get_barrier_semaphore()
+
+    def greet(lat, lev):
+        pl.semaphore_signal(barrier, inc=1, device_id=(lat, lev), device_id_type=MESH)
+
+    column = [(parity * half + lax.rem(lh + off, half), e) for off in range(1, half)]
+    across = (lax.rem(l + half, n_lat), e)
+    partners = [(l, lax.rem(e + off, n_lev)) for off in range(1, n_lev)]
+    partners += column + [across]
+    for there, lat in ((has_down, l + 1), (has_up, l - 1)):
+
+        @pl.when(there)
+        def _():
+            for lev in (e, east, west):
+                greet(lat, lev)
+
+    for lat, lev in partners:
+        greet(lat, lev)
+    n_greet = len(partners) + jnp.where(has_up, 3, 0) + jnp.where(has_down, 3, 0)
+
     def load(k, src, dst):
         copy = pltpu.make_async_copy(src, dst, load_sem.at[k])
         copy.start()
         return copy
 
+    inner_rows = pl.ds(16, rows - 16)
+    inner_field = pl.ds(8, rows - 16)
     for t in range(tiles):
-        load(0, field_hbm.at[:, :, pl.ds(t * LANES, LANES)], ext.at[:, t, pl.ds(8, rows), :])
+        cols = pl.ds(t * LANES, LANES)
+        load(0, field_hbm.at[:, pl.ds(0, 8), cols], ext.at[:, t, pl.ds(8, 8), :])
+        load(0, field_hbm.at[:, pl.ds(rows - 8, 8), cols], ext.at[:, t, pl.ds(rows, 8), :])
+    for t in range(tiles):
+        cols = pl.ds(t * LANES, LANES)
+        k = 8 if t in (0, tiles - 1) else 9
+        for v in range(levels):
+            load(k, field_hbm.at[v, inner_field, cols], ext.at[v, t, inner_rows, :])
     load_leg = load(1, leg_hbm, leg)
     load_slot = load(2, slot_hbm, slot_ref)
     load_wts = load(3, weights_hbm, points.at[pl.ds(0, 4 * rows), :])
@@ -96,26 +125,6 @@
         6, table_hbm.at[:, pl.ds(pl.multiple_of(e * width, LANES), width)], tab
     )
 
-    barrier = pltpu.get_barrier_semaphore()
-
-    def greet(lat, lev):
-        pl.semaphore_signal(barrier, inc=1, device_id=(lat, lev), device_id_type=MESH)
-
-    column = [(parity * half + lax.rem(lh + off, half), e) for off in range(1, half)]
-    across = (lax.rem(l + half, n_lat), e)
-    partners = [(l, lax.rem(e + off, n_lev)) for off in range(1, n_lev)]
-    partners += column + [across]
-    for there, lat in ((has_down, l + 1), (has_up, l - 1)):
-
-        @pl.when(there)
-        def _():
-            for lev in (e, east, west):
-                greet(lat, lev)
-
-    for lat, lev in partners:
-        greet(lat, lev)
-    n_greet = len(partners) + jnp.where(has_up, 3, 0) + jnp.where(has_down, 3, 0)
-
     def tell(k, devices):
         for there in devices:
             pl.semaphore_signal(round_sem.at[k], inc=1, device_id=there, device_id_type=MESH)
@@ -131,10 +140,13 @@
     stage[...] = jnp.zeros_like(stage)
     cross[...] = jnp.zeros_like(cross)
     padded = send_leg.shape[1]
-    basis[:, padded:, :] = jnp.zeros((half, HALF - padded, steps), BF16)
+    basis[:half, padded:, :] = jnp.zeros((half, HALF - padded, steps), BF16)
 
     lane = at((rows, LANES), 1)
-    pltpu.make_async_copy(adv, adv, load_sem.at[0]).wait()
+    outer_part = adv.at[pl.ds(0, 16 * levels), :]
+    pltpu.make_async_copy(outer_part, outer_part, load_sem.at[0]).wait()
+    edge_part = ext.at[:, pl.ds(0, 2), inner_rows, :]
+    pltpu.make_async_copy(edge_part, edge_part, load_sem.at[8]).wait()
     for v in range(levels):
         for t in range(tiles):
             rim_rows[0, t, 2 * v : 2 * v + 2, :] = ext[v, t, 6 + rows : 8 + rows, :]
@@ -189,6 +201,26 @@
 
     tell(0, column)
 
+    if tiles > 2:
+        other_part = ext.at[:, pl.ds(0, tiles - 2), inner_rows, :]
+        pltpu.make_async_copy(other_part, other_part, load_sem.at[9]).wait()
+    load_slot.wait()
+    load_leg.wait()
+    load_tab.wait()
+    load_wts.wait()
+    load_row.wait()
+    load_col.wait()
+    weights_in = rim_inputs.at[pl.ds(0, 64), :]
+    pltpu.make_async_copy(weights_in, weights_in, load_sem.at[7]).wait()
+    first = lax.broadcasted_iota(jnp.int32, (1, 4 * waves), 1)
+    slot_row = jnp.zeros((1, 4 * waves), jnp.int32)
+    for k in range(waves):
+        slot_row = jnp.where(lax.rem(first, waves) == k, slot_ref[k], slot_row)
+    iota_f = (4 * waves, 4 * waves)
+    order = one_hot(
+        (lax.div(at(iota_f, 0), waves) == lax.div(at(iota_f, 1), waves))
+        & (lax.rem(at(iota_f, 0), waves) == slot_row)
+    )
     lane = at((8, LANES), 1)
     moves = (-2, -1, 1, 2)
 
@@ -215,17 +247,6 @@
     for v in range(levels):
         shift_level(v)
 
-    load_slot.wait()
-    first = lax.broadcasted_iota(jnp.int32, (1, 4 * waves), 1)
-    slot_row = jnp.zeros((1, 4 * waves), jnp.int32)
-    for k in range(waves):
-        slot_row = jnp.where(lax.rem(first, waves) == k, slot_ref[k], slot_row)
-    iota_f = (4 * waves, 4 * waves)
-    order = one_hot(
-        (lax.div(at(iota_f, 0), waves) == lax.div(at(iota_f, 1), waves))
-        & (lax.rem(at(iota_f, 0), waves) == slot_row)
-    )
-    load_leg.wait()
     band = 8
     iota_g = (half * band, band * waves)
     slot_cols = jnp.zeros((1, band * waves), jnp.int32)
@@ -242,17 +263,29 @@
         ).astype(BF16)
         for t in range(half):
             send_leg[t, i : i + band, :] = picked[t * band : (t + 1) * band]
-    slots_of = lambda t: basis.at[t, pl.ds(0, padded), :]
-    copies_g = []
-    for off in range(1, half):
-        t = lax.rem(lh + off, half)
-        copy = remote(
-            send_leg.at[t], slots_of(lh), leg_send, leg_recv,
-            parity * half + t, e,
-        )
-        copy.start()
-        copies_g.append(copy)
-    basis[lh, 0:padded, :] = send_leg[lh]
+    tabs[...] = jnp.dot(order, tab[...], preferred_element_type=F32).astype(BF16)
+
+    for q, ref in ((4, drow), (5, dcol)):
+        for k in range(2):
+            row0 = 16 * q + 8 * k
+            rim_inputs[row0 : row0 + 8, :] = (
+                ref[k * (rows - 8) : k * (rows - 8) + 8, :].astype(F32).astype(BF16)
+            )
+        for cols in (slice(0, LANES), slice(width - LANES, width)):
+            points[q * rows : (q + 1) * rows, cols] = ref[:, cols].astype(F32).astype(BF16)
+    iota_r = (6 * 16, 6 * 16)
+    row_r, col_r = at(iota_r, 0), at(iota_r, 1)
+    repeat_rows = one_hot(
+        (lax.div(row_r, 8) == lax.div(col_r, 8))
+        & ((col_r & 7) == (row_r & 1) + jnp.where((row_r & 15) < 8, 0, 6))
+    )
+    rim_points[...] = jnp.dot(repeat_rows, rim_inputs[...], preferred_element_type=F32)
+    row_c, col_c = at((LANES, LANES), 0), at((LANES, LANES), 1)
+    from_first = one_hot((col_c < HALF) & (row_c == (col_c & 1)))
+    from_last = one_hot((col_c >= HALF) & (row_c == LANES - 2 + (col_c & 1)))
+    side_points[...] = jnp.dot(
+        points[:, 0:LANES], from_first, preferred_element_type=F32
+    ) + jnp.dot(points[:, width - LANES :], from_last, preferred_element_type=F32)
 
     def choose_two(high, low, values):
         one = jnp.where(high, values[2], values[0])
@@ -260,9 +293,6 @@
         three = jnp.where(high, values[4], values[2])
         return jnp.where(low, two, one), jnp.where(low, three, two)
 
-    load_wts.wait()
-    load_row.wait()
-    load_col.wait()
 
     sub = at((8, LANES), 0)
 
@@ -311,34 +341,20 @@
     lax.fori_loop(0, tiles // 2, advect, 0)
     pl.semaphore_wait(round_sem.at[0], half - 1)
     tell(1, [across])
+    slots_of = lambda t: basis.at[t, pl.ds(0, padded), :]
+    copies_g = []
+    for off in range(1, half):
+        t = lax.rem(lh + off, half)
+        copy = remote(
+            send_leg.at[t], slots_of(lh), leg_send, leg_recv,
+            parity * half + t, e,
+        )
+        copy.start()
+        copies_g.append(copy)
+    basis[lh, 0:padded, :] = send_leg[lh]
+
+
     lax.fori_loop(tiles // 2, tiles, advect, 0)
-
-    load_tab.wait()
-    tabs[...] = jnp.dot(order, tab[...], preferred_element_type=F32).astype(BF16)
-
-    weights_in = rim_inputs.at[pl.ds(0, 64), :]
-    pltpu.make_async_copy(weights_in, weights_in, load_sem.at[7]).wait()
-    for q, ref in ((4, drow), (5, dcol)):
-        for k in range(2):
-            row0 = 16 * q + 8 * k
-            rim_inputs[row0 : row0 + 8, :] = (
-                ref[k * (rows - 8) : k * (rows - 8) + 8, :].astype(F32).astype(BF16)
-            )
-        for cols in (slice(0, LANES), slice(width - LANES, width)):
-            points[q * rows : (q + 1) * rows, cols] = ref[:, cols].astype(F32).astype(BF16)
-    iota_r = (6 * 16, 6 * 16)
-    row_r, col_r = at(iota_r, 0), at(iota_r, 1)
-    repeat_rows = one_hot(
-        (lax.div(row_r, 8) == lax.div(col_r, 8))
-        & ((col_r & 7) == (row_r & 1) + jnp.where((row_r & 15) < 8, 0, 6))
-    )
-    rim_points[...] = jnp.dot(repeat_rows, rim_inputs[...], preferred_element_type=F32)
-    row_c, col_c = at((LANES, LANES), 0), at((LANES, LANES), 1)
-    from_first = one_hot((col_c < HALF) & (row_c == (col_c & 1)))
-    from_last = one_hot((col_c >= HALF) & (row_c == LANES - 2 + (col_c & 1)))
-    side_points[...] = jnp.dot(
-        points[:, 0:LANES], from_first, preferred_element_type=F32
-    ) + jnp.dot(points[:, width - LANES :], from_last, preferred_element_type=F32)
 
     even = (at((8, LANES), 0) & 1) == 0
 
@@ -510,6 +526,12 @@
     def all_of(ref, sem, count=n - 1):
         return pltpu.make_async_copy(ref.at[pl.ds(0, count)], ref.at[pl.ds(0, count)], sem)
 
+    for b in range(0, half, 2):
+        turned = jnp.dot(
+            flip, basis[b : b + 2].reshape(LANES, steps), preferred_element_type=F32
+        ).astype(BF16)
+        basis[half + b : half + b + 2] = turned.reshape(2, HALF, steps)
+
     all_of(got_1, one_recv).wait()
 
     low = lax.broadcasted_iota(jnp.int32, (lv, LANES), 1) < HALF
@@ -520,37 +542,34 @@
             value = value + got_1[lat * n_lev + d]
         return value
 
-    for b in range(0, half, 2):
-        cols = slice(b * HALF, b * HALF + LANES)
-        for which in range(2):
+    for which in range(2):
+        for b in range(0, half, 2):
             lat = parity * half + b
             one = total_1(lat if which == 0 else n_lat - 1 - lat)
             two = total_1(lat + 1 if which == 0 else n_lat - 2 - lat)
-            row0 = which * 2 * lv
-            both_f[row0 : row0 + lv, cols] = jnp.where(low, one, pltpu.roll(two, HALF, 1))
-            both_f[row0 + lv : row0 + 2 * lv, cols] = jnp.where(
-                low, pltpu.roll(one, HALF, 1), two
-            )
-    near = both_f[0 : 2 * lv, :].astype(BF16)
-    both_b[0 : 2 * lv, :] = near
-    for c0 in range(0, half * HALF, LANES):
-        cols = slice(c0, c0 + LANES)
-        both_b[2 * lv :, cols] = jnp.dot(
-            both_f[2 * lv :, cols].astype(BF16), flip, preferred_element_type=F32
-        ).astype(BF16)
-    matrix = basis[...].reshape(half * HALF, steps)
-    raw = jnp.dot(both_b[...], matrix, preferred_element_type=F32)
-    raw = (raw[2 * lv :] + sign * raw[0 : 2 * lv]) * forward_scale
+            col0 = (which * half + b) * HALF
+            cols = slice(col0, col0 + LANES)
+            both_f[0:lv, cols] = jnp.where(low, one, pltpu.roll(two, HALF, 1))
+            both_f[lv:, cols] = jnp.where(low, pltpu.roll(one, HALF, 1), two)
+    inside = half * HALF
+    terms = both_f[...].astype(BF16)
+    matrix = basis[...].reshape(2 * inside, steps)
+    raw = sign * jnp.dot(
+        terms[:, :inside], matrix[:inside], preferred_element_type=F32
+    ) + jnp.dot(terms[:, inside:], matrix[inside:], preferred_element_type=F32)
+    raw = raw * forward_scale
     masked = jnp.where(degree <= NT, raw, 0.0)
     damped = masked * factor
     change = (damped - masked).astype(BF16)
-    back = lax.dot_general(change, matrix, contract_last, preferred_element_type=F32) * scale
-    both_f[0 : 2 * lv, :] = back
+    back = lax.dot_general(
+        change, matrix[:inside], contract_last, preferred_element_type=F32
+    )
+    both_f[:, :inside] = back * scale
     for b in range(0, half, 2):
         cols = slice(b * HALF, b * HALF + LANES)
-        real, imag = both_f[0:lv, cols], both_f[lv : 2 * lv, cols]
-        send_2[b] = jnp.where(low, real, pltpu.roll(imag, HALF, 1))
-        send_2[b + 1] = jnp.where(low, pltpu.roll(real, HALF, 1), imag)
+        real, imag = both_f[0:lv, cols], both_f[lv:, cols]
+        send_2[b] = jnp.where(low, real, pltpu.roll(imag, HALF, 1)).astype(BF16)
+        send_2[b + 1] = jnp.where(low, pltpu.roll(real, HALF, 1), imag).astype(BF16)
 
     def start_2(lat, lev, owner, block):
         remote(send_2.at[block], got_2.at[me], two_send, two_recv, lat, lev).start()
@@ -581,18 +600,17 @@
     for which in range(2):
         start = jnp.where(which == 1, parity, 1 - parity) * owners
         for o in range(owners):
-            stage[which * pairs + o * lv : which * pairs + (o + 1) * lv, :] = got_2[start + o]
+            stage[which * pairs + o * lv : which * pairs + (o + 1) * lv, :] = got_2[
+                start + o
+            ].astype(F32)
     for which in range(2):
-        value = stage[which * pairs : (which + 1) * pairs, :]
-        lead = value.astype(BF16)
-        rest = (value - lead.astype(F32)).astype(BF16)
+        value = stage[which * pairs : (which + 1) * pairs, :].astype(BF16)
         for c in range(2):
             cols = slice((2 * c + which) * LANES, (2 * c + which + 1) * LANES)
-            cross[0, c * pairs : (c + 1) * pairs, cols] = lead
-            cross[1, c * pairs : (c + 1) * pairs, cols] = rest
+            cross[c * pairs : (c + 1) * pairs, cols] = value
     synth[...] = lax.dot_general(
-        gather, cross[0], contract_last, preferred_element_type=F32
-    ) + lax.dot_general(gather, cross[1], contract_last, preferred_element_type=F32)
+        gather, cross[...], contract_last, preferred_element_type=F32
+    )
 
     keeps = (home == l) & (share == lax.div(e, lv))
     spec_waits = [
@@ -630,7 +648,6 @@
         lead_all[at, :] = jnp.where(level_of == v, lead, 0.0).astype(BF16)
         rest_all[at, :] = jnp.where(level_of == v, rest, 0.0).astype(BF16)
     chunk = min(width, 256)
-    copies = []
     for j in range(0, width, chunk):
         cols = slice(j, j + chunk)
         increment = (
@@ -641,13 +658,11 @@
         updated = adv[:, cols] + increment
         for v in range(levels):
             result[v, :, cols] = updated[v * rows : (v + 1) * rows]
-        copy = pltpu.make_async_copy(
-            result.at[:, :, cols], out_hbm.at[:, :, cols], sems.at[1 + j // chunk]
-        )
-        copy.start()
-        copies.append(copy)
-    for copy in copies + [spec_copy]:
-        copy.wait()
+        pltpu.make_async_copy(
+            result.at[:, :, cols], out_hbm.at[:, :, cols], sems.at[1]
+        ).start()
+    pltpu.make_async_copy(result, out_hbm, sems.at[1]).wait()
+    spec_copy.wait()
 
 
 def solution(mesh):
@@ -697,18 +712,17 @@
                 vmem((6 * rows, LANES), F32),
                 vmem((2, rows + 16, LANES), F32),
                 vmem((half, rows, steps), BF16),
-                vmem((half, HALF, steps), BF16),
+                vmem((n_lat, HALF, steps), BF16),
                 vmem((2 * pairs, LANES), F32),
                 vmem((owners, lv, LANES), F32),
                 vmem((n, lv, LANES), F32),
-                vmem((4 * lv, half * HALF), F32),
-                vmem((4 * lv, half * HALF), BF16),
-                vmem((half, lv, LANES), F32),
-                vmem((n, lv, LANES), F32),
-                vmem((2, 2 * pairs, 4 * LANES), BF16),
+                vmem((2 * lv, n_lat * HALF), F32),
+                vmem((half, lv, LANES), BF16),
+                vmem((n, lv, LANES), BF16),
+                vmem((2 * pairs, 4 * LANES), BF16),
                 vmem((lv, 2, steps), F32),
                 vmem((2 * own, 2, steps), F32),
-                dma((8,)),
+                dma((10,)),
                 dma((3,)), dma((3,)),
                 dma, dma,
                 dma, dma,
@@ -728,7 +742,6 @@
                 )
             ),
         )
-        chunks = width // min(width, 256)
         updated, spectral = pl.pallas_call(
             finish,
             out_shape=(
@@ -741,7 +754,7 @@
                 vmem((levels * rows, 2 * pairs), BF16),
                 vmem((levels * rows, 2 * pairs), BF16),
                 vmem((levels, rows, width), F32),
-                dma((1 + chunks,)),
+                dma((2,)),
             ],
             compiler_params=pltpu.CompilerParams(vmem_limit_bytes=20 << 20),
         )(*(pltpu.with_memory_space_constraint(x, vmem) for x in (adv, synth, wide, spec)))

time: 21.3 us -> 20.9 us (0.981)
  Pallas kernels: 20.5 us -> 20.1 us
    pallas_call x1, Pallas kernels: 19.3 us -> 19 us  [on_device(): pl.pallas_call(functools.partial(kernel, n_lat, n_lev), out_shape=(vmem((...]
where the time goes in v6:
time: 20.9 us; the launch traced here: 20.8 us
  Pallas kernels  20.1 us (96%)
  between operations  0.64 us (3%)
    pallas_call x1, Pallas kernels, on_device(): pl.pallas_call(functools.partial(kernel, n_lat, n_lev), out_shape=(vmem((...  19 us
    pallas_call x1, Pallas kernels, on_device(): pl.pallas_call(finish, out_shape=(jax.ShapeDtypeStruct((levels, rows, wid...  1.15 us

profile of v6, /device:TPU:0, one launch (start us, length us, event | category | flops | bytes accessed | tf_op | source)
XLA Modules:
  0.0 20.8 jit_solution(6276194731210364001)
XLA Ops:
  0.6 19.0 %shard_map.86 = (f32[160,1024]{1,0:T(8,128)S(1)}, f32[40,128]{1,0:T(8,128)S(1)}, bf16[2,128,1024]{2,1,0:T(8,128)(2,1)S(1)}, f32[4,2,640]{2,1,0:T(2,128)S(1)}) custom-call(s32[16]{0:T(128)} %slot_hbm.1, f32[4,40,1024]{2,1,0:T(8,128)} %field_hbm.1, bf16[160,1024]{1,0:T(8,128)(2,1)} %bitcast.6, s32[40,1024]{1,0:T(8,128)} %drow_hbm.1, s32[40,1024]{1,0:T(8,128)} %dcol_hbm.1, ...), custom_call_target="tpu_custom_call" | custom-call | tf_op jit(solution)/shard_map/pallas_call | solution.py:685
  19.6 1.1 %shard_map.87 = (f32[4,40,1024]{2,1,0:T(8,128)}, f32[4,2,640]{2,1,0:T(2,128)}) custom-call(f32[160,1024]{1,0:T(8,128)S(1)} %get-tuple-element.8.adv, f32[40,128]{1,0:T(8,128)S(1)} %get-tuple-element.9.synth, bf16[2,128,1024]{2,1,0:T(8,128)(2,1)S(1)} %get-tuple-element.10.wide, f32[4,2,640]{2,1,0:T(2,128)S(1)} %get-tuple-element.11.spec), custom_call_target="tpu_custom_call" | custom-call | tf_op jit(solution)/shard_map/pallas_call | solution.py:745

commit v7 on v6

--- a/solution.py
+++ b/solution.py
@@ -51,7 +51,7 @@
     adv, synth, wide, spec_ref,
     slot_ref, ext, shifted, points, drow, dcol, leg, tab, tabs,
     rim_rows, pack_row, pack_col, got_rim, got_col, rim_inputs, rim_points, side_points, side,
-    send_leg, basis, stage, send_1, got_1, both_f, send_2, got_2, cross, send_p, got_p,
+    send_leg, basis, stage, split, send_1, got_1, both_f, send_2, got_2, cross, send_p, got_p,
     load_sem, halo_send, halo_recv, leg_send, leg_recv, one_send, one_recv,
     two_send, two_recv, p_send, p_recv, round_sem,
 ):
@@ -107,22 +107,22 @@
         load(0, field_hbm.at[:, pl.ds(rows - 8, 8), cols], ext.at[:, t, pl.ds(rows, 8), :])
     for t in range(tiles):
         cols = pl.ds(t * LANES, LANES)
-        k = 8 if t in (0, tiles - 1) else 9
+        k = 6 if t in (0, tiles - 1) else 7
         for v in range(levels):
             load(k, field_hbm.at[v, inner_field, cols], ext.at[v, t, inner_rows, :])
     load_leg = load(1, leg_hbm, leg)
     load_slot = load(2, slot_hbm, slot_ref)
-    load_wts = load(3, weights_hbm, points.at[pl.ds(0, 4 * rows), :])
+    load(3, weights_hbm, points.at[pl.ds(0, 4 * rows), :])
     for q in range(4):
         for k in range(2):
             load(
-                7, weights_hbm.at[pl.ds(q * rows + k * (rows - 8), 8), :],
+                5, weights_hbm.at[pl.ds(q * rows + k * (rows - 8), 8), :],
                 rim_inputs.at[pl.ds(16 * q + 8 * k, 8), :],
             )
-    load_row = load(4, drow_hbm, drow)
-    load_col = load(5, dcol_hbm, dcol)
+    load(3, drow_hbm, drow)
+    load(3, dcol_hbm, dcol)
     load_tab = load(
-        6, table_hbm.at[:, pl.ds(pl.multiple_of(e * width, LANES), width)], tab
+        4, table_hbm.at[:, pl.ds(pl.multiple_of(e * width, LANES), width)], tab
     )
 
     def tell(k, devices):
@@ -146,7 +146,7 @@
     outer_part = adv.at[pl.ds(0, 16 * levels), :]
     pltpu.make_async_copy(outer_part, outer_part, load_sem.at[0]).wait()
     edge_part = ext.at[:, pl.ds(0, 2), inner_rows, :]
-    pltpu.make_async_copy(edge_part, edge_part, load_sem.at[8]).wait()
+    pltpu.make_async_copy(edge_part, edge_part, load_sem.at[6]).wait()
     for v in range(levels):
         for t in range(tiles):
             rim_rows[0, t, 2 * v : 2 * v + 2, :] = ext[v, t, 6 + rows : 8 + rows, :]
@@ -178,8 +178,8 @@
     rims = [
         [
             halo(k, pack_row.at[k], got_rim.at[k, pl.ds(1, tiles)], lat, e),
-            halo(k, pack_row.at[k, tiles - 1], got_rim.at[k, 0], lat, east),
-            halo(k, pack_row.at[k, 0], got_rim.at[k, tiles + 1], lat, west),
+            halo(3 + k, pack_row.at[k, tiles - 1], got_rim.at[k, 0], lat, east),
+            halo(3 + k, pack_row.at[k, 0], got_rim.at[k, tiles + 1], lat, west),
         ]
         for k, lat in ((0, l + 1), (1, l - 1))
     ]
@@ -203,15 +203,14 @@
 
     if tiles > 2:
         other_part = ext.at[:, pl.ds(0, tiles - 2), inner_rows, :]
-        pltpu.make_async_copy(other_part, other_part, load_sem.at[9]).wait()
+        pltpu.make_async_copy(other_part, other_part, load_sem.at[7]).wait()
     load_slot.wait()
     load_leg.wait()
     load_tab.wait()
-    load_wts.wait()
-    load_row.wait()
-    load_col.wait()
+    point_part = adv.at[pl.ds(0, 4 * rows), :]
+    pltpu.make_async_copy(point_part, point_part, load_sem.at[3]).wait()
     weights_in = rim_inputs.at[pl.ds(0, 64), :]
-    pltpu.make_async_copy(weights_in, weights_in, load_sem.at[7]).wait()
+    pltpu.make_async_copy(weights_in, weights_in, load_sem.at[5]).wait()
     first = lax.broadcasted_iota(jnp.int32, (1, 4 * waves), 1)
     slot_row = jnp.zeros((1, 4 * waves), jnp.int32)
     for k in range(waves):
@@ -358,18 +357,21 @@
 
     even = (at((8, LANES), 0) & 1) == 0
 
-    def fix_rows(k):
+    def fix_rows(k, first_tile, last_tile):
         for c0 in range(0, 2 * levels, 8):
-            blocks = [got_rim[k, t, c0 : c0 + 8, :].astype(F32) for t in range(tiles + 2)]
+            blocks = [
+                got_rim[k, t, c0 : c0 + 8, :].astype(F32)
+                for t in range(first_tile, last_tile + 3)
+            ]
             moved = [move_blocks(blocks, move) for move in moves]
             moved.insert(2, blocks[1:-1])
-            for t in range(tiles):
+            for t in range(first_tile, last_tile + 1):
                 cols = slice(t * LANES, (t + 1) * LANES)
                 w0, w1, w2, w3, dr, dc = [
                     rim_points[16 * q + 8 * k : 16 * q + 8 * k + 8, cols] for q in range(6)
                 ]
                 col_high, col_low = dc >= 0.0, (dc == -1.0) | (dc == 1.0)
-                same = [moved[c][t] for c in range(5)]
+                same = [moved[c][t - first_tile] for c in range(5)]
                 other = [pltpu.roll(x, 1 if k else 7, 0) for x in same]
                 s0, s1 = choose_two(col_high, col_low, same)
                 o0, o1 = choose_two(col_high, col_low, other)
@@ -392,15 +394,15 @@
                     row0 = (c0 + i) // 2 * rows + k * (rows - 2)
                     adv[row0 : row0 + 2, cols] += extra[i : i + 2]
 
-    @pl.when(has_up)
-    def _():
-        pltpu.make_async_copy(got_rim.at[0], got_rim.at[0], halo_recv.at[0]).wait()
-        fix_rows(0)
-
-    @pl.when(has_down)
-    def _():
-        pltpu.make_async_copy(got_rim.at[1], got_rim.at[1], halo_recv.at[1]).wait()
-        fix_rows(1)
+    rim_middle = [got_rim.at[k, pl.ds(1, tiles)] for k in range(2)]
+    rim_corner = [got_rim.at[k, pl.ds(0, 2)] for k in range(2)]
+    for k, there in ((0, has_up), (1, has_down)):
+
+        @pl.when(there)
+        def _():
+            pltpu.make_async_copy(rim_middle[k], rim_middle[k], halo_recv.at[k]).wait()
+            if tiles > 2:
+                fix_rows(k, 1, tiles - 2)
 
     pltpu.make_async_copy(got_col, got_col, halo_recv.at[2]).wait()
     here = jnp.where(
@@ -441,18 +443,34 @@
             east_part = pltpu.roll(extra, (LANES - 2 - HALF - 2 * v) % LANES, 1)
             adv[band, width - LANES :] += jnp.where(lane >= LANES - 2, east_part, 0.0)
 
+    for k, there in ((0, has_up), (1, has_down)):
+
+        @pl.when(there)
+        def _():
+            pltpu.make_async_copy(rim_corner[k], rim_corner[k], halo_recv.at[3 + k]).wait()
+            fix_rows(k, 0, 0)
+            fix_rows(k, tiles - 1, tiles - 1)
+
     contract_last = (((1,), (1,)), ((), ()))
-    for v in range(levels):
-        value = adv[v * rows : (v + 1) * rows, :]
-        lead = value.astype(BF16)
-        rest = (value - lead.astype(F32)).astype(BF16)
-        both = lax.dot_general(tabs[...], lead, contract_last, preferred_element_type=F32)
+    for pair in range(levels // 2):
+        for k in range(2):
+            v = 2 * pair + k
+            value = adv[v * rows : (v + 1) * rows, :]
+            lead = value.astype(BF16)
+            split[pair, k * rows : (k + 1) * rows, :] = lead
+            split[pair, (2 + k) * rows : (3 + k) * rows, :] = (
+                value - lead.astype(F32)
+            ).astype(BF16)
+        both = lax.dot_general(
+            tabs[...], split[pair, 0 : 2 * rows, :], contract_last, preferred_element_type=F32
+        )
         more = lax.dot_general(
-            tabs[0 : 2 * waves, :], rest, contract_last, preferred_element_type=F32
-        )
-        coeffs = both[0 : 2 * waves] + both[2 * waves :] + more
-        stage[v * waves : (v + 1) * waves, 0:rows] = coeffs[0:waves]
-        stage[v * waves : (v + 1) * waves, HALF : HALF + rows] = coeffs[waves:]
+            tabs[0 : 2 * waves, :], split[pair, 2 * rows :, :], contract_last,
+            preferred_element_type=F32,
+        )
+        stage[2 * waves * pair : 2 * waves * (pair + 1), 0 : 2 * rows] = (
+            both[0 : 2 * waves] + both[2 * waves :] + more
+        )
     owners = half * n_lev
     for s in range(waves):
         for g in range(rep):
@@ -487,7 +505,10 @@
 
     spread_rows = 2 * waves * levels
     iota_w = (spread_rows, 2 * waves)
-    repeat = one_hot(lax.div(at(iota_w, 0), levels) == at(iota_w, 1))
+    row_w = at(iota_w, 0)
+    repeat = one_hot(
+        (row_w & 1) * waves + lax.div(lax.rem(row_w, waves * levels), levels) == at(iota_w, 1)
+    )
     for q in range(2):
         wide[q] = jnp.dot(
             repeat, tabs[2 * waves * q : 2 * waves * (q + 1), :], preferred_element_type=F32
@@ -550,7 +571,9 @@
             col0 = (which * half + b) * HALF
             cols = slice(col0, col0 + LANES)
             both_f[0:lv, cols] = jnp.where(low, one, pltpu.roll(two, HALF, 1))
-            both_f[lv:, cols] = jnp.where(low, pltpu.roll(one, HALF, 1), two)
+            both_f[lv:, cols] = jnp.where(
+                low, pltpu.roll(one, LANES - rows, 1), pltpu.roll(two, HALF - rows, 1)
+            )
     inside = half * HALF
     terms = both_f[...].astype(BF16)
     matrix = basis[...].reshape(2 * inside, steps)
@@ -580,7 +603,8 @@
 
     for vv in range(lv):
         for c in range(2):
-            send_p[vv, c : c + 1, :] = damped[c * lv + vv : c * lv + vv + 1]
+            row0 = lv * (vv % 2) + 2 * (vv // 2) + c
+            send_p[vv, c : c + 1, :] = damped[row0 : row0 + 1]
     home, place_p = lax.div(slot, own), lax.rem(slot, own)
     for vv in range(lv):
         lev = share * lv + vv
@@ -630,9 +654,8 @@
     pl.when(jnp.logical_not(keeps))(all_of(send_p, p_send, lv).wait)
 
     for k, there in ((0, has_down), (1, has_up)):
-        pl.when(there)(
-            pltpu.make_async_copy(got_rim.at[k], got_rim.at[k], halo_send.at[k]).wait
-        )
+        for ref, sem in ((rim_middle[k], halo_send.at[k]), (rim_corner[k], halo_send.at[3 + k])):
+            pl.when(there)(pltpu.make_async_copy(ref, ref, sem).wait)
 
 
 def finish(adv, synth, wide, spec, out_hbm, spec_hbm, lead_all, rest_all, result, sems):
@@ -642,7 +665,9 @@
     value = synth[...]
     lead = value.astype(BF16).astype(F32)
     rest = value - lead
-    level_of = lax.rem(lax.broadcasted_iota(jnp.int32, value.shape, 1), levels)
+    column = lax.broadcasted_iota(jnp.int32, value.shape, 1)
+    level_of = lax.rem(column, levels)
+    level_of = level_of - (level_of & 1) + lax.div(column, value.shape[1] // 2)
     for v in range(levels):
         at = slice(v * rows, (v + 1) * rows)
         lead_all[at, :] = jnp.where(level_of == v, lead, 0.0).astype(BF16)
@@ -714,6 +739,7 @@
                 vmem((half, rows, steps), BF16),
                 vmem((n_lat, HALF, steps), BF16),
                 vmem((2 * pairs, LANES), F32),
+                vmem((levels // 2, 4 * rows, width), BF16),
                 vmem((owners, lv, LANES), F32),
                 vmem((n, lv, LANES), F32),
                 vmem((2 * lv, n_lat * HALF), F32),
@@ -722,8 +748,8 @@
                 vmem((2 * pairs, 4 * LANES), BF16),
                 vmem((lv, 2, steps), F32),
                 vmem((2 * own, 2, steps), F32),
-                dma((10,)),
-                dma((3,)), dma((3,)),
+                dma((8,)),
+                dma((5,)), dma((5,)),
                 dma, dma,
                 dma, dma,
                 dma, dma,

time: 20.9 us -> 20.8 us (level)
  no operation moved by 1% of the time
where the time goes in v7:
time: 20.8 us; the launch traced here: 20.6 us
  Pallas kernels  20 us (96%)
  between operations  0.64 us (3%)
    pallas_call x1, Pallas kernels, on_device(): pl.pallas_call(functools.partial(kernel, n_lat, n_lev), out_shape=(vmem((...  18.8 us
    pallas_call x1, Pallas kernels, on_device(): pl.pallas_call(finish, out_shape=(jax.ShapeDtypeStruct((levels, rows, wid...  1.15 us

profile of v7, /device:TPU:0, one launch (start us, length us, event | category | flops | bytes accessed | tf_op | source)
XLA Modules:
  0.0 20.6 jit_solution(6645772484333010671)
XLA Ops:
  0.6 18.8 %shard_map.86 = (f32[160,1024]{1,0:T(8,128)S(1)}, f32[40,128]{1,0:T(8,128)S(1)}, bf16[2,128,1024]{2,1,0:T(8,128)(2,1)S(1)}, f32[4,2,640]{2,1,0:T(2,128)S(1)}) custom-call(s32[16]{0:T(128)} %slot_hbm.1, f32[4,40,1024]{2,1,0:T(8,128)} %field_hbm.1, bf16[160,1024]{1,0:T(8,128)(2,1)} %bitcast.6, s32[40,1024]{1,0:T(8,128)} %drow_hbm.1, s32[40,1024]{1,0:T(8,128)} %dcol_hbm.1, ...), custom_call_target="tpu_custom_call" | custom-call | tf_op jit(solution)/shard_map/pallas_call | solution.py:710
  19.5 1.2 %shard_map.87 = (f32[4,40,1024]{2,1,0:T(8,128)}, f32[4,2,640]{2,1,0:T(2,128)}) custom-call(f32[160,1024]{1,0:T(8,128)S(1)} %get-tuple-element.8.adv, f32[40,128]{1,0:T(8,128)S(1)} %get-tuple-element.9.synth, bf16[2,128,1024]{2,1,0:T(8,128)(2,1)S(1)} %get-tuple-element.10.wide, f32[4,2,640]{2,1,0:T(2,128)S(1)} %get-tuple-element.11.spec), custom_call_target="tpu_custom_call" | custom-call | tf_op jit(solution)/shard_map/pallas_call | solution.py:771

commit v8 on v7

--- a/solution.py
+++ b/solution.py
@@ -394,16 +394,6 @@
                     row0 = (c0 + i) // 2 * rows + k * (rows - 2)
                     adv[row0 : row0 + 2, cols] += extra[i : i + 2]
 
-    rim_middle = [got_rim.at[k, pl.ds(1, tiles)] for k in range(2)]
-    rim_corner = [got_rim.at[k, pl.ds(0, 2)] for k in range(2)]
-    for k, there in ((0, has_up), (1, has_down)):
-
-        @pl.when(there)
-        def _():
-            pltpu.make_async_copy(rim_middle[k], rim_middle[k], halo_recv.at[k]).wait()
-            if tiles > 2:
-                fix_rows(k, 1, tiles - 2)
-
     pltpu.make_async_copy(got_col, got_col, halo_recv.at[2]).wait()
     here = jnp.where(
         at((rows, LANES), 1) < HALF, got_col[0].astype(F32), got_col[1].astype(F32)
@@ -442,6 +432,16 @@
             adv[band, 0:LANES] += jnp.where(lane < 2, west_part, 0.0)
             east_part = pltpu.roll(extra, (LANES - 2 - HALF - 2 * v) % LANES, 1)
             adv[band, width - LANES :] += jnp.where(lane >= LANES - 2, east_part, 0.0)
+
+    rim_middle = [got_rim.at[k, pl.ds(1, tiles)] for k in range(2)]
+    rim_corner = [got_rim.at[k, pl.ds(0, 2)] for k in range(2)]
+    for k, there in ((0, has_up), (1, has_down)):
+
+        @pl.when(there)
+        def _():
+            pltpu.make_async_copy(rim_middle[k], rim_middle[k], halo_recv.at[k]).wait()
+            if tiles > 2:
+                fix_rows(k, 1, tiles - 2)
 
     for k, there in ((0, has_up), (1, has_down)):
 
@@ -476,26 +476,26 @@
         for g in range(rep):
             send_1[s * rep + g] = stage[pl.ds(g * lv * waves + s, lv, stride=waves), :]
 
-    turn_by = jnp.where(parity == 0, n_lat - 1, 1)
+    by_distance = sorted(range(n_lev), key=lambda b: -min(b, n_lev - b))
 
     def others(body):
-        def column_of(a, first):
-            lat = lax.rem(l + turn_by * a, n_lat)
+        def column_of(a):
+            lat = jnp.where(parity == 0, n_lat - 1 - a, a)
             inside = lax.div(lat, half) == parity
             block = jnp.where(inside, lat, n_lat - 1 - lat) - parity * half
             base = lax.rem(lat, half) * n_lev
-
-            def send(b):
+            for b in by_distance:
                 lev = lax.rem(e + b, n_lev)
-                body(lat, lev, base + lev, block)
-
-            each(first, n_lev)(send)
-
-        each(1, n_lat)(lambda a: column_of(a, 0))
-        column_of(0, 1)
+                copy = body(lat, lev, base + lev, block)
+                if b:
+                    copy.start()
+                else:
+                    pl.when(lat != l)(copy.start)
+
+        each(0, n_lat)(column_of)
 
     def start_1(lat, lev, owner, block):
-        remote(send_1.at[owner], got_1.at[me], one_send, one_recv, lat, lev).start()
+        return remote(send_1.at[owner], got_1.at[me], one_send, one_recv, lat, lev)
 
     pl.semaphore_wait(round_sem.at[1], 1)
 
@@ -595,7 +595,7 @@
         send_2[b + 1] = jnp.where(low, pltpu.roll(real, HALF, 1), imag).astype(BF16)
 
     def start_2(lat, lev, owner, block):
-        remote(send_2.at[block], got_2.at[me], two_send, two_recv, lat, lev).start()
+        return remote(send_2.at[block], got_2.at[me], two_send, two_recv, lat, lev)
 
     others(start_2)
 

time: 20.8 us -> 20.7 us (level)
  no operation moved by 1% of the time
where the time goes in v8:
time: 20.7 us; the launch traced here: 20.5 us
  Pallas kernels  19.9 us (96%)
  between operations  0.64 us (3%)
    pallas_call x1, Pallas kernels, on_device(): pl.pallas_call(functools.partial(kernel, n_lat, n_lev), out_shape=(vmem((...  18.7 us
    pallas_call x1, Pallas kernels, on_device(): pl.pallas_call(finish, out_shape=(jax.ShapeDtypeStruct((levels, rows, wid...  1.15 us

profile of v8, /device:TPU:0, one launch (start us, length us, event | category | flops | bytes accessed | tf_op | source)
XLA Modules:
  0.0 20.5 jit_solution(2240242015022918585)
XLA Ops:
  0.6 18.7 %shard_map.86 = (f32[160,1024]{1,0:T(8,128)S(1)}, f32[40,128]{1,0:T(8,128)S(1)}, bf16[2,128,1024]{2,1,0:T(8,128)(2,1)S(1)}, f32[4,2,640]{2,1,0:T(2,128)S(1)}) custom-call(s32[16]{0:T(128)} %slot_hbm.1, f32[4,40,1024]{2,1,0:T(8,128)} %field_hbm.1, bf16[160,1024]{1,0:T(8,128)(2,1)} %bitcast.6, s32[40,1024]{1,0:T(8,128)} %drow_hbm.1, s32[40,1024]{1,0:T(8,128)} %dcol_hbm.1, ...), custom_call_target="tpu_custom_call" | custom-call | tf_op jit(solution)/shard_map/pallas_call | solution.py:710
  19.4 1.1 %shard_map.87 = (f32[4,40,1024]{2,1,0:T(8,128)}, f32[4,2,640]{2,1,0:T(2,128)}) custom-call(f32[160,1024]{1,0:T(8,128)S(1)} %get-tuple-element.8.adv, f32[40,128]{1,0:T(8,128)S(1)} %get-tuple-element.9.synth, bf16[2,128,1024]{2,1,0:T(8,128)(2,1)S(1)} %get-tuple-element.10.wide, f32[4,2,640]{2,1,0:T(2,128)S(1)} %get-tuple-element.11.spec), custom_call_target="tpu_custom_call" | custom-call | tf_op jit(solution)/shard_map/pallas_call | solution.py:771
